TPU v7x, 256 devices: a whole 4x4x8 slice. The times are simulated.
256 devices in a mesh: gx: 8 (over x, core), gy: 4 (over y), gz: 8 (over z).
Axes of the slice: x: 4, y: 4, z: 8, core: 2. Of those that a mesh axis runs over, the one named last changes fastest.
Arguments:
- left_core: float32 [256, 4096, 256], P(None, ('gx', 'gy', 'gz')), may hold values from -4000 to 4000
- right_core: float32 [256, 4096, 256], P(None, ('gx', 'gy', 'gz')), may hold values from -0.00012207031 to 0.00012207031
Outputs:
- left_out: float32 [256, 4096, 128], P(None, ('gx', 'gy', 'gz'))
- right_out: float32 [128, 4096, 256], P(None, ('gx', 'gy', 'gz'))
- next_factor: float32 [256, 256], replicated
All inputs are finite; a program needn't handle non-finite values.
Results may differ from a plain program's by a relative error of at most 0.000075.
Values sent between devices are 32-bit elements; how exact they have to be, the bound alone decides.
A program may use at most 192 MiB of HBM per device.

v0:
```python
import math

import jax
import jax.numpy as jnp
from jax import lax
from jax.sharding import PartitionSpec as P

RK = 128


def gram_of(matrix_rows):
    return lax.dot_general(
        matrix_rows,
        matrix_rows,
        (((0,), (0,)), ((), ())),
        precision=lax.Precision.HIGHEST,
        preferred_element_type=jnp.float32,
    )


def per_device(left_core, right_core):
    rank_left, points_local, rank_mid = left_core.shape
    rank_right = right_core.shape[2]
    total_points = points_local * lax.axis_size("gx") * lax.axis_size("gy") * lax.axis_size("gz")
    unfold = left_core.reshape(rank_left * points_local, rank_mid)
    lower_one = jnp.linalg.cholesky(lax.psum(gram_of(unfold), ("gx", "gy", "gz")))
    upper_full = lower_one.T
    ortho_cols = lax.linalg.triangular_solve(
        lower_one[:RK, :RK], unfold[:, :RK], left_side=False, lower=True, transpose_a=True
    )
    left_out = (ortho_cols * math.sqrt(rank_left * total_points)).reshape(
        rank_left, points_local, RK
    )
    absorbed = jnp.dot(
        upper_full[:RK, :],
        right_core.reshape(rank_mid, points_local * rank_right),
        precision=lax.Precision.HIGHEST,
        preferred_element_type=jnp.float32,
    )
    summed = lax.psum(gram_of(absorbed.reshape(RK * points_local, rank_right)), ("gx", "gy", "gz"))
    factor = jnp.linalg.cholesky(summed / (RK * total_points)).T
    right_out = absorbed.reshape(RK, points_local, rank_right)
    return (left_out, right_out, factor)


def solution(mesh):
    in_specs = (P(None, ("gx", "gy", "gz"), None), P(None, ("gx", "gy", "gz"), None))
    out_specs = (P(None, ("gx", "gy", "gz"), None), P(None, ("gx", "gy", "gz"), None), P())
    return jax.shard_map(
        per_device, mesh=mesh, in_specs=in_specs, out_specs=out_specs, check_vma=False
    )
```

profile of v0, /device:TPU:1, one launch (start us, length us, event | category | flops | bytes accessed | tf_op | source)
XLA Modules:
  0.0 617.1 jit_solution(7845188268302011180)
XLA Ops:
  7.2 0.0 all-reduce.4.cloned.1.call-start
  7.2 10.9 %convolution_bitcast_fusion = f32[256,256]{0,1:T(8,128)} fusion(f32[256,16,256]{2,1,0:T(8,128)} %param.3), kind=kOutput, calls=%fused_computation.3 | convolution fusion | flops 3221225472 | bytes 4456448 | tf_op jit(solution)/shard_map/dot_general | solution.py:12
  18.1 0.0 all-reduce.4.cloned.1.call-update
  18.1 0.5 all-reduce.6.cloned.1.call-start
  18.6 7.9 %copy.26 = f32[32,8,16,256]{3,1,2,0:T(8,128)} copy(f32[32,8,16,256]{3,2,1,0:T(8,128)} %bitcast.53) | data formatting | bytes 8388608
  26.5 244.4 %all-reduce.4.cloned.1.call-done = f32[256,256]{0,1:T(8,128)} async-done(((f32[256,256]{0,1:T(8,128)}), f32[256,256]{0,1:T(8,128)}) %all-reduce.4.cloned.1.call-update) | async-done | bytes 262160 | tf_op jit(solution)/shard_map/psum | solution.py:26
  270.9 1.1 copy.16
  272.0 1.0 fusion.3
  273.0 11.7 %cholesky.130 = f32[128,128]{1,0:T(8,128)S(1)} custom-call(f32[128,128]{1,0:T(8,128)S(1)} %cholesky.194), custom_call_target="Cholesky" | custom-call | tf_op jit(solution)/shard_map/jit(cholesky)/cholesky | solution.py:26
  284.7 9.8 %custom-call.13 = f32[1,128,128]{1,2,0:T(8,128)S(1)} custom-call(f32[1,128,128]{2,1,0:T(8,128)S(1)} %get-tuple-element.17), custom_call_target="InvertDiagBlocksLowerTriangular" | custom-call | tf_op jit(solution)/shard_map/jit(cholesky)/cholesky | solution.py:26
  294.6 0.2 constant_dynamic-update-slice_fusion.3
  294.8 0.3 convolution_subtract_fusion.1
  295.1 11.9 %cholesky.147 = f32[128,128]{1,0:T(8,128)S(1)} custom-call(f32[128,128]{1,0:T(8,128)S(1)} %convolution_subtract_fusion.1), custom_call_target="Cholesky" | custom-call | tf_op jit(solution)/shard_map/jit(cholesky)/cholesky | solution.py:26
  307.0 0.6 compare_reduce_fusion.2
  309.0 4.5 fusion.4
  313.5 1.5 reshape.39
  315.0 6.4 %fusion.14 = f32[256,256]{0,1:T(8,128)} fusion(f32[2048,256]{1,0:T(8,128)} %reshape.39), kind=kOutput, calls=%fused_computation.41 | convolution fusion | flops 1610612736 | bytes 2359296 | tf_op jit(solution)/shard_map/dot_general | solution.py:12
  321.4 0.0 all-reduce.6.cloned.1.call-update
  321.4 9.8 %custom-call.11 = f32[1,128,128]{1,2,0:T(8,128)S(1)} custom-call(f32[1,128,128]{2,1,0:T(8,128)S(1)} %fusion.8), custom_call_target="InvertDiagBlocksLowerTriangular" | custom-call | tf_op jit(solution)/shard_map/triangular_solve | solution.py:28
  331.2 4.9 fusion
  336.1 2.0 copy.27
  338.1 3.1 copy.17
  341.2 229.4 %all-reduce.6.cloned.1.call-done = f32[256,256]{0,1:T(8,128)} async-done(((f32[256,256]{0,1:T(8,128)}), f32[256,256]{0,1:T(8,128)}) %all-reduce.6.cloned.1.call-update) | async-done | bytes 262160 | tf_op jit(solution)/shard_map/psum | solution.py:40
  570.5 1.0 broadcast_multiply_fusion
  571.5 0.1 copy.19
  571.6 1.0 fusion.2
  572.6 11.7 %cholesky.164 = f32[128,128]{1,0:T(8,128)S(1)} custom-call(f32[128,128]{1,0:T(8,128)S(1)} %cholesky.197), custom_call_target="Cholesky" | custom-call | tf_op jit(solution)/shard_map/jit(cholesky)/cholesky | solution.py:41
  584.4 9.8 %custom-call.14 = f32[1,128,128]{1,2,0:T(8,128)S(1)} custom-call(f32[1,128,128]{2,1,0:T(8,128)S(1)} %get-tuple-element.13), custom_call_target="InvertDiagBlocksLowerTriangular" | custom-call | tf_op jit(solution)/shard_map/jit(cholesky)/cholesky | solution.py:41
  594.2 0.2 constant_dynamic-update-slice_fusion.1
  594.4 0.3 convolution_subtract_fusion
  594.7 11.7 %cholesky.181 = f32[128,128]{1,0:T(8,128)S(1)} custom-call(f32[128,128]{1,0:T(8,128)S(1)} %convolution_subtract_fusion), custom_call_target="Cholesky" | custom-call | tf_op jit(solution)/shard_map/jit(cholesky)/cholesky | solution.py:41
  606.4 0.7 compare_reduce_fusion
  607.2 0.6 compare_reduce_fusion.1
  609.2 0.8 copy.20
  (12 shorter events, 0.3 us)
Async XLA Ops:
  7.2 263.7 %all-reduce.4.cloned.1.call-start = ((), (), s32[]{:S(2)}) async-start(), calls=%async_computation | async-start | bytes 524288 | tf_op jit(solution)/shard_map/psum | solution.py:26
  18.1 552.4 %all-reduce.6.cloned.1.call-start = ((), (), s32[]{:S(2)}) async-start(), calls=%async_computation.1 | async-start | bytes 524288 | tf_op jit(solution)/shard_map/psum | solution.py:40
Sparse Core Ops, SparseCore 0:
  18.2 252.6 all-reduce.3
  321.5 248.9 all-reduce.5
where the time goes:
time: 623 us; the launch traced here: 617 us
  waiting for transfers between devices  474 us (76%)
  other arithmetic  81.6 us (13%)
  matrix products  27.6 us (4%)
  between operations  17.1 us (3%)
  local copies, waits for them, and re-layouts  16.5 us (3%)
    psum x1, waiting for transfers between devices, per_device(): lax.psum(gram_of(unfold), ('gx', 'gy', 'gz'))  244 us
    psum x1, waiting for transfers between devices, per_device(): lax.psum(gram_of(absorbed.reshape(RK * points_local, rank_right)), ('gx',...  229 us
    another operation x7, other arithmetic, per_device(): factor = jnp.linalg.cholesky(summed / (RK * total_points)).T  34.7 us
    another operation x6, other arithmetic, per_device(): jnp.linalg.cholesky(lax.psum(gram_of(unfold), ('gx', 'gy', 'gz')))  34.1 us
    dot_general x2, matrix products, gram_of(): lax.dot_general(matrix_rows, matrix_rows, (((0,), (0,)), ((), ())), preci...  17.3 us
  transfers between devices with their start and end apart: 2, of which 2 were waited for; matrix products, arithmetic and copies ran while one was open for 4% of the time, Pallas kernels for 0%

commit v1 on v0

v1 whole, which is shorter than its diff:
```python
import functools

import jax
import jax.numpy as jnp
from jax import lax
from jax.experimental import pallas as pl
from jax.experimental.pallas import tpu as pltpu
from jax.sharding import PartitionSpec as P

RK = 128
F32 = jnp.float32
BF16 = jnp.bfloat16
MESH = pl.DeviceIdType.MESH


def split(x):
    hi = x.astype(BF16)
    return hi, (x - hi.astype(F32)).astype(BF16)


def mm(a, b):
    return lax.dot_general(a, b, (((1,), (0,)), ((), ())), preferred_element_type=F32)


def mm_tn(a, b):
    return lax.dot_general(a, b, (((0,), (0,)), ((), ())), preferred_element_type=F32)


def gram_kernel(steps, x_ref, out_ref, acc, acc_lo):
    step = pl.program_id(0)
    hi, lo = split(x_ref[...])
    main = mm_tn(jnp.concatenate([hi[:, :RK], lo[:, :RK]], axis=1), hi)
    cross = mm_tn(hi[:, :RK], lo)
    part = main[:RK] + (main[RK:] + cross)

    @pl.when(step == 0)
    def _():
        acc[...] = part

    @pl.when(step > 0)
    def _():
        acc[...] += part

    @pl.when(step == steps - 1)
    def _():
        for half in range(2):
            out_ref[half * 16 : half * 16 + 16] = acc[:, half * RK : half * RK + RK].reshape(16, 1, 8, 128)


def local_gram(unfold):
    rows, cols = unfold.shape
    steps = 4
    return pl.pallas_call(
        functools.partial(gram_kernel, steps),
        grid=(steps,),
        out_shape=jax.ShapeDtypeStruct((32, 1, 8, 128), F32),
        in_specs=[pl.BlockSpec((rows // steps, cols), lambda i: (i, 0))],
        out_specs=pl.BlockSpec((32, 1, 8, 128), lambda i: (0, 0, 0, 0)),
        scratch_shapes=[pltpu.VMEM((RK, cols), F32), pltpu.VMEM((8, 128), F32)],
        compiler_params=pltpu.CompilerParams(vmem_limit_bytes=48 << 20),
        name="local_gram",
    )(unfold)


def sum_kernel(nx, ny, nz, src_ref, out_ref, rx, rz, s1, r1, s2, r2, s3, r3):
    gx, gy, gz = lax.axis_index("gx"), lax.axis_index("gy"), lax.axis_index("gz")
    n = nx * ny
    me = gx * ny + gy

    def plane(step):
        k = lax.rem(me + step, n)
        return k, (lax.div(k, ny), lax.rem(k, ny), gz)

    def line(step):
        return (gx, gy, lax.rem(gz + step, nz))

    barrier = pltpu.get_barrier_semaphore()

    @pl.loop(1, n)
    def _(s):
        pl.semaphore_signal(barrier, inc=1, device_id=plane(s)[1], device_id_type=MESH)

    @pl.loop(1, nz)
    def _(s):
        pl.semaphore_signal(barrier, inc=1, device_id=line(s), device_id_type=MESH)

    pl.semaphore_wait(barrier, n - 1 + nz - 1)

    def scatter(s):
        k, dev = plane(s)
        return pltpu.make_async_remote_copy(
            src_ref.at[k], rx.at[s], s1.at[s], r1.at[s], device_id=dev, device_id_type=MESH
        )

    def across(s):
        return pltpu.make_async_remote_copy(
            rz.at[gz], rz.at[gz], s2.at[s], r2.at[s], device_id=line(s), device_id_type=MESH
        )

    def gather(s):
        return pltpu.make_async_remote_copy(
            out_ref.at[me], out_ref.at[me], s3.at[s], r3.at[s], device_id=plane(s)[1], device_id_type=MESH
        )

    @pl.loop(1, n)
    def _(s):
        scatter(s).start()

    def take(s, acc):
        scatter(s).wait_recv()
        return acc + rx[s]

    rz[gz] = lax.fori_loop(1, n, take, src_ref[me])

    @pl.loop(1, nz)
    def _(s):
        across(s).start()

    @pl.loop(1, nz)
    def _(s):
        across(s).wait_recv()

    total = rz[0]
    for z in range(1, nz):
        total = total + rz[z]
    out_ref[me] = total

    @pl.loop(1, n)
    def _(s):
        gather(s).start()

    @pl.loop(1, n)
    def _(s):
        scatter(s).wait_send()

    @pl.loop(1, nz)
    def _(s):
        across(s).wait_send()

    @pl.loop(1, n)
    def _(s):
        gather(s).wait_recv()

    @pl.loop(1, n)
    def _(s):
        gather(s).wait_send()


def device_sum(src, sizes, ident):
    nx, ny, nz = sizes
    n = nx * ny
    tiles = src.shape[1]
    dma = pltpu.SemaphoreType.DMA
    return pl.pallas_call(
        functools.partial(sum_kernel, nx, ny, nz),
        out_shape=jax.ShapeDtypeStruct(src.shape, F32),
        in_specs=[pl.BlockSpec(memory_space=pltpu.VMEM)],
        out_specs=pl.BlockSpec(memory_space=pltpu.VMEM),
        scratch_shapes=[
            pltpu.VMEM((n, tiles, 8, 128), F32),
            pltpu.VMEM((nz, tiles, 8, 128), F32),
            dma((n,)), dma((n,)), dma((nz,)), dma((nz,)), dma((n,)), dma((n,)),
        ],
        compiler_params=pltpu.CompilerParams(collective_id=ident, has_side_effects=True),
        name="device_sum",
    )(src)


def rsqrt(x):
    r = lax.rsqrt(x)
    return r * (1.5 - 0.5 * x * r * r)


def eliminate(work, tiles):
    shape = (8, 128)
    for b in range(16):
        r0 = 8 * b
        rows8 = pl.ds(r0, 8)
        panel = [work[rows8, 128 * t : 128 * t + 128] for t in range(tiles)]

        def lanes(x):
            return [jnp.broadcast_to(x[:, r0 + k : r0 + k + 1], shape) for k in range(8)]

        cols = lanes(panel[0])
        e = [[jnp.broadcast_to(cols[k][i : i + 1, :], shape) if k <= i else None for k in range(8)] for i in range(8)]
        rows = [[jnp.broadcast_to(p[i : i + 1, :], shape) for i in range(8)] for p in panel]
        scale, mult = [], []
        for i in range(8):
            rs = rsqrt(e[i][i])
            l = [None] * 8
            for k in range(i + 1, 8):
                l[k] = e[k][i] * rs
            for k in range(i + 1, 8):
                for j in range(k, 8):
                    e[j][k] = e[j][k] - l[j] * l[k]
            scale.append(rs)
            mult.append(l)

        def apply(v):
            v = list(v)
            for i in range(8):
                v[i] = v[i] * scale[i]
                for k in range(i + 1, 8):
                    v[k] = v[k] - mult[i][k] * v[i]
            return v

        rows = [apply(r) for r in rows]
        sub = lax.broadcasted_iota(jnp.int32, shape, 0)
        for t in range(tiles):
            out = rows[t][0]
            for i in range(1, 8):
                out = jnp.where(sub == i, rows[t][i], out)
            work[rows8, 128 * t : 128 * t + 128] = out
        for m in range(b + 1, 16):
            m8 = pl.ds(8 * m, 8)
            cm = apply(lanes(work[m8, 0:128]))
            for t in range(tiles):
                v = work[m8, 128 * t : 128 * t + 128]
                for k in range(8):
                    v = v - cm[k] * rows[t][k]
                work[m8, 128 * t : 128 * t + 128] = v


def upper_mask():
    return lax.broadcasted_iota(jnp.int32, (128, 128), 0) <= lax.broadcasted_iota(jnp.int32, (128, 128), 1)


def identity():
    return jnp.where(
        lax.broadcasted_iota(jnp.int32, (128, 128), 0) == lax.broadcasted_iota(jnp.int32, (128, 128), 1), 1.0, 0.0
    ).astype(F32)


def cores_kernel(points, root, norm, g_ref, left_hbm, right_hbm, lo_hbm, ro_hbm, g2_ref,
                 work, lbuf, rbuf, lout, rout, sem):
    gets = [pltpu.make_async_copy(right_hbm.at[:, 128 * h : 128 * h + 128], rbuf.at[h], sem.at[h]) for h in range(2)]
    get_left = pltpu.make_async_copy(left_hbm.at[:, 0:128], lbuf, sem.at[4])
    for get in gets:
        get.start()
    get_left.start()
    work[:, 0:128] = g_ref[0:16].reshape(128, 128)
    work[:, 128:256] = g_ref[16:32].reshape(128, 128)
    work[:, 256:384] = identity()
    eliminate(work, 3)
    upper = jnp.concatenate([jnp.where(upper_mask(), work[:, 0:128], 0.0), work[:, 128:256]], axis=1)
    up_hi, up_lo = split(upper)
    up_both = jnp.concatenate([up_hi, up_lo], axis=0)
    for get in gets:
        get.wait()
    g_main = jnp.zeros((256, 256), F32)
    g_cross = jnp.zeros((256, 256), F32)
    for pair in range(points // 2):
        both = []
        for p in (2 * pair, 2 * pair + 1):
            at = pl.ds(p, 256, stride=points)
            r_hi, r_lo = split(jnp.concatenate([rbuf[0, at, :], rbuf[1, at, :]], axis=1))
            main = mm(up_both, r_hi)
            o = main[:128] + (main[128:] + mm(up_hi, r_lo))
            for h in range(2):
                rout[h, pl.ds(p, 128, stride=points), :] = o[:, 128 * h : 128 * h + 128]
            both.append(o)
        o_hi, o_lo = split(jnp.concatenate(both, axis=0))
        g_main = g_main + mm_tn(o_hi, o_hi)
        g_cross = g_cross + mm_tn(o_hi, o_lo)
    puts = [pltpu.make_async_copy(rout.at[h], ro_hbm.at[:, 128 * h : 128 * h + 128], sem.at[2 + h]) for h in range(2)]
    for put in puts:
        put.start()
    gram = (g_main + (g_cross + g_cross.T)) * norm
    for half in range(2):
        g2_ref[:, half] = gram[:, 128 * half : 128 * half + 128].reshape(32, 8, 128)
    w_hi, w_lo = split(work[:, 256:384].T * root)
    weights = jnp.concatenate(
        [jnp.concatenate([w_hi, w_lo], axis=1), jnp.concatenate([w_hi, jnp.zeros_like(w_lo)], axis=1)], axis=0
    )
    get_left.wait()
    rows = lbuf.shape[0]
    chunks = 4
    size = rows // chunks
    for c in range(chunks):
        at = pl.ds(c * size, size)
        x_hi, x_lo = split(lbuf[at, :])
        y = mm(jnp.concatenate([x_hi, x_lo], axis=1), weights)
        lout[at, :] = y[:, :128] + y[:, 128:]
        puts.append(pltpu.make_async_copy(lout.at[at, :], lo_hbm.at[at, :], sem.at[5 + c]))
        puts[-1].start()
    for put in puts:
        put.wait()


def new_cores(gram, left, right, points, root, norm):
    rows = left.shape[0]
    out_rows = RK * points
    any_spec = pl.BlockSpec(memory_space=pl.ANY)
    vmem_spec = pl.BlockSpec(memory_space=pltpu.VMEM)
    return pl.pallas_call(
        functools.partial(cores_kernel, points, root, norm),
        out_shape=(
            jax.ShapeDtypeStruct((rows, RK), F32),
            jax.ShapeDtypeStruct((out_rows, 256), F32),
            jax.ShapeDtypeStruct((32, 2, 8, 128), F32),
        ),
        in_specs=[vmem_spec, any_spec, any_spec],
        out_specs=(any_spec, any_spec, vmem_spec),
        scratch_shapes=[
            pltpu.VMEM((128, 384), F32),
            pltpu.VMEM((rows, RK), F32),
            pltpu.VMEM((2, right.shape[0], 128), F32),
            pltpu.VMEM((rows, RK), F32),
            pltpu.VMEM((2, out_rows, 128), F32),
            pltpu.SemaphoreType.DMA((9,)),
        ],
        compiler_params=pltpu.CompilerParams(vmem_limit_bytes=48 << 20),
        name="new_cores",
    )(gram, left, right)


def factor_kernel(g_ref, out_ref, work):
    work[:, 0:128] = g_ref[0:16, 0].reshape(128, 128)
    work[:, 128:256] = g_ref[0:16, 1].reshape(128, 128)
    eliminate(work, 2)
    right = work[:, 128:256]
    out_ref[0:128, 0:128] = jnp.where(upper_mask(), work[:, 0:128], 0.0)
    out_ref[0:128, 128:256] = right
    update = lax.dot_general(
        right, right, (((0,), (0,)), ((), ())), precision=lax.Precision.HIGHEST, preferred_element_type=F32
    )
    work[:, 0:128] = g_ref[16:32, 1].reshape(128, 128) - update
    eliminate(work, 1)
    out_ref[128:256, 0:128] = jnp.zeros((128, 128), F32)
    out_ref[128:256, 128:256] = jnp.where(upper_mask(), work[:, 0:128], 0.0)


def upper_factor(gram):
    return pl.pallas_call(
        factor_kernel,
        out_shape=jax.ShapeDtypeStruct((256, 256), F32),
        in_specs=[pl.BlockSpec(memory_space=pltpu.VMEM)],
        out_specs=pl.BlockSpec(memory_space=pltpu.VMEM),
        scratch_shapes=[pltpu.VMEM((128, 256), F32)],
        name="upper_factor",
    )(gram)


def per_device(left_core, right_core, sizes):
    rank_left, points, rank_mid = left_core.shape
    rank_right = right_core.shape[2]
    total_points = points * sizes[0] * sizes[1] * sizes[2]
    left = left_core.reshape(rank_left * points, rank_mid)
    right = right_core.reshape(rank_mid * points, rank_right)
    gram = device_sum(local_gram(left), sizes, 0)
    gram = gram.reshape(32, 8, 128)
    root = float(rank_left * total_points) ** 0.5
    norm = 1.0 / (RK * total_points)
    left_out, right_out, gram2 = new_cores(gram, left, right, points, root, norm)
    factor = upper_factor(device_sum(gram2, sizes, 1))
    return (
        left_out.reshape(rank_left, points, RK),
        right_out.reshape(RK, points, rank_right),
        factor,
    )


def solution(mesh):
    sizes = tuple(mesh.shape[a] for a in ("gx", "gy", "gz"))
    spec = P(None, ("gx", "gy", "gz"), None)
    return jax.shard_map(
        functools.partial(per_device, sizes=sizes),
        mesh=mesh, in_specs=(spec, spec), out_specs=(spec, spec, P()), check_vma=False,
    )
```

time: 623 us -> 84.6 us (0.14)
  waiting for transfers between devices: 474 us -> 0 us
  other arithmetic: 81.6 us -> 0 us
  Pallas kernels: 0 us -> 77 us
  matrix products: 27.6 us -> 0 us
  between operations: 17.1 us -> 0.7 us
  local copies, waits for them, and re-layouts: 16.5 us -> 6.62 us
    psum x2 -> x0, waiting for transfers between devices: 474 us -> none  [the longest x1 244 us: per_device(): lax.psum(gram_of(unfold), ('gx', 'gy', 'gz'))]
    another operation x15 -> x0, other arithmetic: 78.6 us -> none  [the longest x7 34.7 us: per_device(): factor = jnp.linalg.cholesky(summed / (RK * total_points)).T]
    pallas_call x0 -> x5, Pallas kernels: none -> 77 us  [the longest x2 52.7 us: device_sum(): pl.pallas_call(functools.partial(sum_kernel, nx, ny, nz), out_shape=jax.S...]
    dot_general x3 -> x0, matrix products: 21.8 us -> none  [the longest x2 17.3 us: gram_of(): lax.dot_general(matrix_rows, matrix_rows, (((0,), (0,)), ((), ())), preci...]
  transfers between devices with their start and end apart: 2 -> 0, of which waited for: 2 -> 0; matrix products, arithmetic and copies ran while one was open for 4% -> 0% of each run, Pallas kernels for 0% -> 0%
where the time goes in v1:
time: 84.6 us; the launch traced here: 84.4 us
  Pallas kernels  77 us (91%)
  local copies, waits for them, and re-layouts  6.62 us (8%)
    pallas_call x2, Pallas kernels, device_sum(): pl.pallas_call(functools.partial(sum_kernel, nx, ny, nz), out_shape=jax.S...  52.7 us
    pallas_call x1, Pallas kernels, upper_factor(): pl.pallas_call(factor_kernel, out_shape=jax.ShapeDtypeStruct((256, 256),...  11.4 us
    pallas_call x1, Pallas kernels, new_cores(): pl.pallas_call(functools.partial(cores_kernel, points, root, norm), out_s...  11.2 us
    unnamed x10, local copies, waits for them, and re-layouts  6.62 us
    pallas_call x1, Pallas kernels, local_gram(): pl.pallas_call(functools.partial(gram_kernel, steps), grid=(steps,), out_...  1.77 us

profile of v1, /device:TPU:1, one launch (start us, length us, event | category | flops | bytes accessed | tf_op | source)
XLA Modules:
  0.0 84.4 jit_solution(7649399349345280961)
XLA Ops:
  0.6 0.0 copy-start
  0.6 2.2 %copy-done = f32[256,16,256]{2,1,0:T(8,128)S(1)} copy-done((f32[256,16,256]{2,1,0:T(8,128)S(1)}, f32[256,16,256]{2,1,0:T(8,128)}, u32[]{:S(2)}) %copy-start) | copy-done | bytes 4194328
  2.8 1.8 %local_gram.1.src_ref = f32[32,1,8,128]{3,2,1,0:T(8,128)S(1)} custom-call(f32[4096,256]{1,0:T(8,128)S(1)} %bitcast.5), custom_call_target="tpu_custom_call" | custom-call | tf_op jit(solution)/shard_map/local_gram/pallas_call | solution.py:53
  4.6 0.0 copy-start.3
  4.6 0.6 copy-done.3
  5.3 29.0 %device_sum.2 = f32[32,1,8,128]{3,2,1,0:T(8,128)} custom-call(f32[32,1,8,128]{3,2,1,0:T(8,128)} %copy-done.3), custom_call_target="tpu_custom_call" | custom-call | tf_op jit(solution)/shard_map/device_sum/pallas_call | solution.py:154
  34.2 0.0 copy-start.1
  34.3 2.2 %copy-done.1 = f32[256,16,256]{2,1,0:T(8,128)S(1)} copy-done((f32[256,16,256]{2,1,0:T(8,128)S(1)}, f32[256,16,256]{2,1,0:T(8,128)}, u32[]{:S(2)}) %copy-start.1) | copy-done | bytes 4194328
  36.4 0.0 copy-start.2
  36.4 0.9 %copy-done.2 = f32[32,1,8,128]{3,2,1,0:T(8,128)S(1)} copy-done((f32[32,1,8,128]{3,2,1,0:T(8,128)S(1)}, f32[32,1,8,128]{3,2,1,0:T(8,128)}, u32[]{:S(2)}) %copy-start.2) | copy-done | bytes 131096
  37.3 11.2 %new_cores.1 = (f32[4096,128]{1,0:T(8,128)}, f32[2048,256]{1,0:T(8,128)}, f32[32,2,8,128]{3,2,1,0:T(8,128)S(1)}) custom-call(f32[32,8,128]{2,1,0:T(8,128)S(1)} %bitcast.7, f32[4096,256]{1,0:T(8,128)S(1)} %bitcast.6, f32[4096,256]{1,0:T(8,128)} %bitcast.8), custom_call_target="tpu_custom_call" | custom-call | tf_op jit(solution)/shard_map/new_cores/pallas_call | solution.py:295
  48.5 0.0 copy-start.4
  48.5 0.7 copy-done.4
  49.2 23.8 %device_sum.3.g_ref = f32[32,2,8,128]{3,2,1,0:T(8,128)} custom-call(f32[32,2,8,128]{3,2,1,0:T(8,128)} %copy-done.4), custom_call_target="tpu_custom_call" | custom-call | tf_op jit(solution)/shard_map/device_sum/pallas_call | solution.py:154
  73.0 11.4 %upper_factor.1 = f32[256,256]{1,0:T(8,128)} custom-call(f32[32,2,8,128]{3,2,1,0:T(8,128)} %device_sum.3.g_ref), custom_call_target="tpu_custom_call" | custom-call | tf_op jit(solution)/shard_map/upper_factor/pallas_call | solution.py:334
Async XLA Ops:
  0.6 2.2 %copy-start = (f32[256,16,256]{2,1,0:T(8,128)S(1)}, f32[256,16,256]{2,1,0:T(8,128)}, u32[]{:S(2)}) copy-start(f32[256,16,256]{2,1,0:T(8,128)} %param.2) | copy-start | bytes 12582916
  4.6 0.7 copy-start.3
  34.2 2.2 %copy-start.1 = (f32[256,16,256]{2,1,0:T(8,128)S(1)}, f32[256,16,256]{2,1,0:T(8,128)}, u32[]{:S(2)}) copy-start(f32[256,16,256]{2,1,0:T(8,128)} %param.2) | copy-start | bytes 12582916
  36.4 0.9 %copy-start.2 = (f32[32,1,8,128]{3,2,1,0:T(8,128)S(1)}, f32[32,1,8,128]{3,2,1,0:T(8,128)}, u32[]{:S(2)}) copy-start(f32[32,1,8,128]{3,2,1,0:T(8,128)} %device_sum.2) | copy-start | bytes 393220
  48.5 0.7 copy-start.4

commit v2 on v1

v2 whole, which is shorter than its diff:
```python
import functools

import jax
import jax.numpy as jnp
from jax import lax
from jax.experimental import pallas as pl
from jax.experimental.pallas import tpu as pltpu
from jax.sharding import PartitionSpec as P

RK = 128
F32 = jnp.float32
BF16 = jnp.bfloat16
MESH = pl.DeviceIdType.MESH


def split(x):
    hi = x.astype(BF16)
    return hi, (x - hi.astype(F32)).astype(BF16)


def mm(a, b):
    return lax.dot_general(a, b, (((1,), (0,)), ((), ())), preferred_element_type=F32)


def mm_tn(a, b):
    return lax.dot_general(a, b, (((0,), (0,)), ((), ())), preferred_element_type=F32)


def exchange(sizes, src, out, rx, rz, sems, meanwhile):
    nx, ny, nz = sizes
    gx, gy, gz = lax.axis_index("gx"), lax.axis_index("gy"), lax.axis_index("gz")
    n = nx * ny
    me = gx * ny + gy

    def scatter(s):
        k, dev = plane(sizes, s)
        return pltpu.make_async_remote_copy(
            src.at[k], rx.at[s], sems.at[0, s], sems.at[1, s], device_id=dev, device_id_type=MESH
        )

    def across(s):
        return pltpu.make_async_remote_copy(
            rz.at[gz], rz.at[gz], sems.at[2, s], sems.at[3, s], device_id=line(sizes, s), device_id_type=MESH
        )

    def gather(s):
        return pltpu.make_async_remote_copy(
            out.at[me], out.at[me], sems.at[4, s], sems.at[5, s], device_id=plane(sizes, s)[1], device_id_type=MESH
        )

    @pl.loop(1, n)
    def _(s):
        scatter(s).start()

    meanwhile()

    def take(s, acc):
        scatter(s).wait_recv()
        return acc + rx[s]

    rz[gz] = lax.fori_loop(1, n, take, src[me])

    @pl.loop(1, nz)
    def _(s):
        across(s).start()

    @pl.loop(1, nz)
    def _(s):
        across(s).wait_recv()

    total = rz[0]
    for z in range(1, nz):
        total = total + rz[z]
    out[me] = total

    @pl.loop(1, n)
    def _(s):
        gather(s).start()

    @pl.loop(1, n)
    def _(s):
        gather(s).wait_recv()

    def finish():
        @pl.loop(1, n)
        def _(s):
            scatter(s).wait_send()
            gather(s).wait_send()

        @pl.loop(1, nz)
        def _(s):
            across(s).wait_send()

    return finish


def plane(sizes, step):
    n = sizes[0] * sizes[1]
    k = lax.rem(lax.axis_index("gx") * sizes[1] + lax.axis_index("gy") + step, n)
    return k, (lax.div(k, sizes[1]), lax.rem(k, sizes[1]), lax.axis_index("gz"))


def line(sizes, step):
    return (lax.axis_index("gx"), lax.axis_index("gy"), lax.rem(lax.axis_index("gz") + step, sizes[2]))


def rsqrt(x):
    r = lax.rsqrt(x)
    return r * (1.5 - 0.5 * x * r * r)


def eliminate(work, tiles):
    shape = (8, 128)
    for b in range(16):
        r0 = 8 * b
        rows8 = pl.ds(r0, 8)
        panel = [work[rows8, 128 * t : 128 * t + 128] for t in range(tiles)]

        def lanes(x):
            return [jnp.broadcast_to(x[:, r0 + k : r0 + k + 1], shape) for k in range(8)]

        cols = lanes(panel[0])
        e = [[jnp.broadcast_to(cols[k][i : i + 1, :], shape) if k <= i else None for k in range(8)] for i in range(8)]
        rows = [[jnp.broadcast_to(p[i : i + 1, :], shape) for i in range(8)] for p in panel]
        scale, mult = [], []
        for i in range(8):
            rs = rsqrt(e[i][i])
            l = [None] * 8
            for k in range(i + 1, 8):
                l[k] = e[k][i] * rs
            for k in range(i + 1, 8):
                for j in range(k, 8):
                    e[j][k] = e[j][k] - l[j] * l[k]
            scale.append(rs)
            mult.append(l)

        def apply(v):
            v = list(v)
            for i in range(8):
                v[i] = v[i] * scale[i]
                for k in range(i + 1, 8):
                    v[k] = v[k] - mult[i][k] * v[i]
            return v

        rows = [apply(r) for r in rows]
        sub = lax.broadcasted_iota(jnp.int32, shape, 0)
        for t in range(tiles):
            out = rows[t][0]
            for i in range(1, 8):
                out = jnp.where(sub == i, rows[t][i], out)
            work[rows8, 128 * t : 128 * t + 128] = out
        for m in range(b + 1, 16):
            m8 = pl.ds(8 * m, 8)
            cm = apply(lanes(work[m8, 0:128]))
            for t in range(tiles):
                v = work[m8, 128 * t : 128 * t + 128]
                for k in range(8):
                    v = v - cm[k] * rows[t][k]
                work[m8, 128 * t : 128 * t + 128] = v


def upper_mask():
    return lax.broadcasted_iota(jnp.int32, (128, 128), 0) <= lax.broadcasted_iota(jnp.int32, (128, 128), 1)


def identity():
    return jnp.where(
        lax.broadcasted_iota(jnp.int32, (128, 128), 0) == lax.broadcasted_iota(jnp.int32, (128, 128), 1), 1.0, 0.0
    ).astype(F32)


def whole_kernel(sizes, points, root, norm, left_hbm, right_hbm, lo_hbm, ro_hbm, f_ref,
                 lbuf, rbuf, r_hi, r_lo, lout, rout, work, src1, sum1, rx1, rz1, src2, sum2, rx2, rz2,
                 sems1, sems2, sem):
    nx, ny, nz = sizes
    rows = lbuf.shape[0]
    chunks = 4
    size = rows // chunks
    spans = [pl.ds(c * size, size) for c in range(chunks)]
    get_left = [pltpu.make_async_copy(left_hbm.at[at, :], lbuf.at[at, :], sem.at[c]) for c, at in enumerate(spans)]
    get_right = [
        pltpu.make_async_copy(right_hbm.at[:, 128 * h : 128 * h + 128], rbuf.at[h], sem.at[4 + h]) for h in range(2)
    ]
    for get in get_left + get_right:
        get.start()

    barrier = pltpu.get_barrier_semaphore()

    @pl.loop(1, nx * ny)
    def _(s):
        pl.semaphore_signal(barrier, inc=1, device_id=plane(sizes, s)[1], device_id_type=MESH)

    @pl.loop(1, nz)
    def _(s):
        pl.semaphore_signal(barrier, inc=1, device_id=line(sizes, s), device_id_type=MESH)

    gram = jnp.zeros((RK, 256), F32)
    for get, at in zip(get_left, spans):
        get.wait()
        hi, lo = split(lbuf[at, :])
        main = mm_tn(jnp.concatenate([hi[:, :RK], lo[:, :RK]], axis=1), hi)
        gram = gram + (main[:RK] + (main[RK:] + mm_tn(hi[:, :RK], lo)))
    for half in range(2):
        src1[half * 16 : half * 16 + 16] = gram[:, half * RK : half * RK + RK].reshape(16, 1, 8, 128)

    pl.semaphore_wait(barrier, nx * ny - 1 + nz - 1)

    def prepare_right():
        for get in get_right:
            get.wait()
        for p in range(points):
            at = pl.ds(p, 256, stride=points)
            for h in range(2):
                hi, lo = split(rbuf[h, at, :])
                r_hi[p, :, 128 * h : 128 * h + 128] = hi
                r_lo[p, :, 128 * h : 128 * h + 128] = lo

    finish1 = exchange(sizes, src1, sum1, rx1, rz1, sems1, prepare_right)

    work[:, 0:128] = sum1[0:16].reshape(128, 128)
    work[:, 128:256] = sum1[16:32].reshape(128, 128)
    work[:, 256:384] = identity()
    eliminate(work, 3)
    upper = jnp.concatenate([jnp.where(upper_mask(), work[:, 0:128], 0.0), work[:, 128:256]], axis=1)
    up_hi, up_lo = split(upper)
    up_both = jnp.concatenate([up_hi, up_lo], axis=0)
    g_main = jnp.zeros((256, 256), F32)
    g_cross = jnp.zeros((256, 256), F32)
    for pair in range(points // 2):
        both = []
        for p in (2 * pair, 2 * pair + 1):
            main = mm(up_both, r_hi[p])
            o = main[:128] + (main[128:] + mm(up_hi, r_lo[p]))
            for h in range(2):
                rout[h, pl.ds(p, 128, stride=points), :] = o[:, 128 * h : 128 * h + 128]
            both.append(o)
        o_hi, o_lo = split(jnp.concatenate(both, axis=0))
        g_main = g_main + mm_tn(o_hi, o_hi)
        g_cross = g_cross + mm_tn(o_hi, o_lo)
    put_right = [
        pltpu.make_async_copy(rout.at[h], ro_hbm.at[:, 128 * h : 128 * h + 128], sem.at[6 + h]) for h in range(2)
    ]
    for put in put_right:
        put.start()
    gram = (g_main + (g_cross + g_cross.T)) * norm
    for half in range(2):
        src2[:, half] = gram[:, 128 * half : 128 * half + 128].reshape(32, 8, 128)

    put_left = [pltpu.make_async_copy(lout.at[at, :], lo_hbm.at[at, :], sem.at[8 + c]) for c, at in enumerate(spans)]

    def make_left():
        w_hi, w_lo = split(work[:, 256:384].T * root)
        weights = jnp.concatenate(
            [jnp.concatenate([w_hi, w_lo], axis=1), jnp.concatenate([w_hi, jnp.zeros_like(w_lo)], axis=1)], axis=0
        )
        for put, at in zip(put_left, spans):
            x_hi, x_lo = split(lbuf[at, 0:128])
            y = mm(jnp.concatenate([x_hi, x_lo], axis=1), weights)
            lout[at, :] = y[:, :128] + y[:, 128:]
            put.start()

    finish2 = exchange(sizes, src2, sum2, rx2, rz2, sems2, make_left)

    work[:, 0:128] = sum2[0:16, 0].reshape(128, 128)
    work[:, 128:256] = sum2[0:16, 1].reshape(128, 128)
    eliminate(work, 2)
    right = work[:, 128:256]
    f_ref[0:128, 0:128] = jnp.where(upper_mask(), work[:, 0:128], 0.0)
    f_ref[0:128, 128:256] = right
    update = lax.dot_general(
        right, right, (((0,), (0,)), ((), ())), precision=lax.Precision.HIGHEST, preferred_element_type=F32
    )
    work[:, 0:128] = sum2[16:32, 1].reshape(128, 128) - update
    eliminate(work, 1)
    f_ref[128:256, 0:128] = jnp.zeros((128, 128), F32)
    f_ref[128:256, 128:256] = jnp.where(upper_mask(), work[:, 0:128], 0.0)
    for put in put_right + put_left:
        put.wait()
    finish1()
    finish2()


def whole(left, right, sizes, points, root, norm):
    rows = left.shape[0]
    out_rows = RK * points
    n, nz = sizes[0] * sizes[1], sizes[2]
    any_spec = pl.BlockSpec(memory_space=pl.ANY)
    return pl.pallas_call(
        functools.partial(whole_kernel, sizes, points, root, norm),
        out_shape=(
            jax.ShapeDtypeStruct((rows, RK), F32),
            jax.ShapeDtypeStruct((out_rows, 256), F32),
            jax.ShapeDtypeStruct((256, 256), F32),
        ),
        in_specs=[any_spec, any_spec],
        out_specs=(any_spec, any_spec, pl.BlockSpec(memory_space=pltpu.VMEM)),
        scratch_shapes=[
            pltpu.VMEM((rows, 256), F32),
            pltpu.VMEM((2, right.shape[0], 128), F32),
            pltpu.VMEM((points, 256, 256), BF16),
            pltpu.VMEM((points, 256, 256), BF16),
            pltpu.VMEM((rows, RK), F32),
            pltpu.VMEM((2, out_rows, 128), F32),
            pltpu.VMEM((128, 384), F32),
            pltpu.VMEM((32, 1, 8, 128), F32),
            pltpu.VMEM((32, 1, 8, 128), F32),
            pltpu.VMEM((n, 1, 8, 128), F32),
            pltpu.VMEM((nz, 1, 8, 128), F32),
            pltpu.VMEM((32, 2, 8, 128), F32),
            pltpu.VMEM((32, 2, 8, 128), F32),
            pltpu.VMEM((n, 2, 8, 128), F32),
            pltpu.VMEM((nz, 2, 8, 128), F32),
            pltpu.SemaphoreType.DMA((6, n)),
            pltpu.SemaphoreType.DMA((6, n)),
            pltpu.SemaphoreType.DMA((12,)),
        ],
        compiler_params=pltpu.CompilerParams(
            collective_id=0, has_side_effects=True, vmem_limit_bytes=56 << 20
        ),
        name="whole",
    )(left, right)


def per_device(left_core, right_core, sizes):
    rank_left, points, rank_mid = left_core.shape
    rank_right = right_core.shape[2]
    total_points = points * sizes[0] * sizes[1] * sizes[2]
    left = left_core.reshape(rank_left * points, rank_mid)
    right = right_core.reshape(rank_mid * points, rank_right)
    root = float(rank_left * total_points) ** 0.5
    norm = 1.0 / (RK * total_points)
    left_out, right_out, factor = whole(left, right, sizes, points, root, norm)
    return (
        left_out.reshape(rank_left, points, RK),
        right_out.reshape(RK, points, rank_right),
        factor,
    )


def solution(mesh):
    sizes = tuple(mesh.shape[a] for a in ("gx", "gy", "gz"))
    spec = P(None, ("gx", "gy", "gz"), None)
    return jax.shard_map(
        functools.partial(per_device, sizes=sizes),
        mesh=mesh, in_specs=(spec, spec), out_specs=(spec, spec, P()), check_vma=False,
    )
```

time: 84.6 us -> 71.5 us (0.85)
  Pallas kernels: 77 us -> 65.5 us
  local copies, waits for them, and re-layouts: 6.62 us -> 5.22 us
    pallas_call x5 -> x1, Pallas kernels: 77 us -> 65.5 us  [whole(): pl.pallas_call(functools.partial(whole_kernel, sizes, points, root, norm)...]
    unnamed x10 -> x7, local copies, waits for them, and re-layouts: 6.62 us -> 5.22 us
where the time goes in v2:
time: 71.5 us; the launch traced here: 71.4 us
  Pallas kernels  65.5 us (92%)
  local copies, waits for them, and re-layouts  5.22 us (7%)
    pallas_call x1, Pallas kernels, whole(): pl.pallas_call(functools.partial(whole_kernel, sizes, points, root, norm)...  65.5 us
    unnamed x7, local copies, waits for them, and re-layouts  5.22 us

profile of v2, /device:TPU:1, one launch (start us, length us, event | category | flops | bytes accessed | tf_op | source)
XLA Modules:
  0.0 71.4 jit_solution(9854714361376589292)
XLA Ops:
  0.6 65.5 %whole.1 = (f32[4096,128]{1,0:T(8,128)}, f32[2048,256]{1,0:T(8,128)}, f32[256,256]{1,0:T(8,128)}) custom-call(f32[4096,256]{1,0:T(8,128)} %bitcast.4, f32[4096,256]{1,0:T(8,128)} %bitcast.5), custom_call_target="tpu_custom_call" | custom-call | tf_op jit(solution)/shard_map/whole/pallas_call | solution.py:288
  66.2 0.0 copy-start
  66.2 3.2 %copy.8 = f32[256,16,128]{2,1,0:T(8,128)} copy(f32[256,16,128]{2,1,0:T(8,128)} %bitcast.7) | data formatting | bytes 4194304
  69.4 0.0 copy-done
  69.4 0.0 copy-start.1
  69.4 1.3 %copy.9 = f32[128,16,256]{2,1,0:T(8,128)} copy(f32[128,16,256]{2,1,0:T(8,128)S(1)} %bitcast.6) | data formatting | bytes 4194304
  70.7 0.0 copy-done.1
  70.7 0.7 copy.10
Async XLA Ops:
  66.2 3.2 %copy-start = (f32[2048,256]{1,0:T(8,128)S(1)}, f32[2048,256]{1,0:T(8,128)}, u32[]{:S(2)}) copy-start(f32[2048,256]{1,0:T(8,128)} %get-tuple-element.7) | copy-start | bytes 6291460
  69.4 1.3 %copy-start.1 = (f32[256,256]{1,0:T(8,128)S(1)}, f32[256,256]{1,0:T(8,128)}, u32[]{:S(2)}) copy-start(f32[256,256]{1,0:T(8,128)} %get-tuple-element.14) | copy-start | bytes 786436

commit v3 on v2

--- a/solution.py
+++ b/solution.py
@@ -104,11 +104,6 @@
     return (lax.axis_index("gx"), lax.axis_index("gy"), lax.rem(lax.axis_index("gz") + step, sizes[2]))
 
 
-def rsqrt(x):
-    r = lax.rsqrt(x)
-    return r * (1.5 - 0.5 * x * r * r)
-
-
 def eliminate(work, tiles):
     shape = (8, 128)
     for b in range(16):
@@ -124,7 +119,7 @@
         rows = [[jnp.broadcast_to(p[i : i + 1, :], shape) for i in range(8)] for p in panel]
         scale, mult = [], []
         for i in range(8):
-            rs = rsqrt(e[i][i])
+            rs = lax.rsqrt(e[i][i])
             l = [None] * 8
             for k in range(i + 1, 8):
                 l[k] = e[k][i] * rs
@@ -169,8 +164,8 @@
     ).astype(F32)
 
 
-def whole_kernel(sizes, points, root, norm, left_hbm, right_hbm, lo_hbm, ro_hbm, f_ref,
-                 lbuf, rbuf, r_hi, r_lo, lout, rout, work, src1, sum1, rx1, rz1, src2, sum2, rx2, rz2,
+def whole_kernel(sizes, points, root, norm, left_hbm, right_hbm, lout, rout, g2_ref,
+                 lbuf, rbuf, r_hi, r_lo, work, src1, sum1, rx1, rz1, src2, sum2, rx2, rz2,
                  sems1, sems2, sem):
     nx, ny, nz = sizes
     rows = lbuf.shape[0]
@@ -237,45 +232,23 @@
         o_hi, o_lo = split(jnp.concatenate(both, axis=0))
         g_main = g_main + mm_tn(o_hi, o_hi)
         g_cross = g_cross + mm_tn(o_hi, o_lo)
-    put_right = [
-        pltpu.make_async_copy(rout.at[h], ro_hbm.at[:, 128 * h : 128 * h + 128], sem.at[6 + h]) for h in range(2)
-    ]
-    for put in put_right:
-        put.start()
     gram = (g_main + (g_cross + g_cross.T)) * norm
     for half in range(2):
         src2[:, half] = gram[:, 128 * half : 128 * half + 128].reshape(32, 8, 128)
-
-    put_left = [pltpu.make_async_copy(lout.at[at, :], lo_hbm.at[at, :], sem.at[8 + c]) for c, at in enumerate(spans)]
 
     def make_left():
         w_hi, w_lo = split(work[:, 256:384].T * root)
         weights = jnp.concatenate(
             [jnp.concatenate([w_hi, w_lo], axis=1), jnp.concatenate([w_hi, jnp.zeros_like(w_lo)], axis=1)], axis=0
         )
-        for put, at in zip(put_left, spans):
+        for at in spans:
             x_hi, x_lo = split(lbuf[at, 0:128])
             y = mm(jnp.concatenate([x_hi, x_lo], axis=1), weights)
             lout[at, :] = y[:, :128] + y[:, 128:]
-            put.start()
 
     finish2 = exchange(sizes, src2, sum2, rx2, rz2, sems2, make_left)
 
-    work[:, 0:128] = sum2[0:16, 0].reshape(128, 128)
-    work[:, 128:256] = sum2[0:16, 1].reshape(128, 128)
-    eliminate(work, 2)
-    right = work[:, 128:256]
-    f_ref[0:128, 0:128] = jnp.where(upper_mask(), work[:, 0:128], 0.0)
-    f_ref[0:128, 128:256] = right
-    update = lax.dot_general(
-        right, right, (((0,), (0,)), ((), ())), precision=lax.Precision.HIGHEST, preferred_element_type=F32
-    )
-    work[:, 0:128] = sum2[16:32, 1].reshape(128, 128) - update
-    eliminate(work, 1)
-    f_ref[128:256, 0:128] = jnp.zeros((128, 128), F32)
-    f_ref[128:256, 128:256] = jnp.where(upper_mask(), work[:, 0:128], 0.0)
-    for put in put_right + put_left:
-        put.wait()
+    g2_ref[...] = sum2[...]
     finish1()
     finish2()
 
@@ -288,19 +261,17 @@
     return pl.pallas_call(
         functools.partial(whole_kernel, sizes, points, root, norm),
         out_shape=(
-            jax.ShapeDtypeStruct((rows, RK), F32),
-            jax.ShapeDtypeStruct((out_rows, 256), F32),
-            jax.ShapeDtypeStruct((256, 256), F32),
+            pltpu.VMEM((rows, RK), F32),
+            pltpu.VMEM((2, out_rows, 128), F32),
+            pltpu.VMEM((32, 2, 8, 128), F32),
         ),
         in_specs=[any_spec, any_spec],
-        out_specs=(any_spec, any_spec, pl.BlockSpec(memory_space=pltpu.VMEM)),
+        out_specs=(pl.BlockSpec(memory_space=pltpu.VMEM),) * 3,
         scratch_shapes=[
             pltpu.VMEM((rows, 256), F32),
             pltpu.VMEM((2, right.shape[0], 128), F32),
             pltpu.VMEM((points, 256, 256), BF16),
             pltpu.VMEM((points, 256, 256), BF16),
-            pltpu.VMEM((rows, RK), F32),
-            pltpu.VMEM((2, out_rows, 128), F32),
             pltpu.VMEM((128, 384), F32),
             pltpu.VMEM((32, 1, 8, 128), F32),
             pltpu.VMEM((32, 1, 8, 128), F32),
@@ -312,13 +283,54 @@
             pltpu.VMEM((nz, 2, 8, 128), F32),
             pltpu.SemaphoreType.DMA((6, n)),
             pltpu.SemaphoreType.DMA((6, n)),
-            pltpu.SemaphoreType.DMA((12,)),
+            pltpu.SemaphoreType.DMA((6,)),
         ],
         compiler_params=pltpu.CompilerParams(
             collective_id=0, has_side_effects=True, vmem_limit_bytes=56 << 20
         ),
         name="whole",
     )(left, right)
+
+
+def factor_kernel(g_ref, lo_in, ro_in, f_ref, lo_out, ro_out, work, sem):
+    puts = [pltpu.make_async_copy(lo_in, lo_out, sem.at[2])]
+    for h in range(2):
+        puts.append(pltpu.make_async_copy(ro_in.at[h], ro_out.at[:, 128 * h : 128 * h + 128], sem.at[h]))
+    for put in puts:
+        put.start()
+    work[:, 0:128] = g_ref[0:16, 0].reshape(128, 128)
+    work[:, 128:256] = g_ref[0:16, 1].reshape(128, 128)
+    eliminate(work, 2)
+    right = work[:, 128:256]
+    f_ref[0:128, 0:128] = jnp.where(upper_mask(), work[:, 0:128], 0.0)
+    f_ref[0:128, 128:256] = right
+    update = lax.dot_general(
+        right, right, (((0,), (0,)), ((), ())), precision=lax.Precision.HIGHEST, preferred_element_type=F32
+    )
+    work[:, 0:128] = g_ref[16:32, 1].reshape(128, 128) - update
+    eliminate(work, 1)
+    f_ref[128:256, 0:128] = jnp.zeros((128, 128), F32)
+    f_ref[128:256, 128:256] = jnp.where(upper_mask(), work[:, 0:128], 0.0)
+    for put in puts:
+        put.wait()
+
+
+def factor_and_place(gram, left_out, right_out):
+    hbm_spec = pl.BlockSpec(memory_space=pltpu.HBM)
+    vmem_spec = pl.BlockSpec(memory_space=pltpu.VMEM)
+    return pl.pallas_call(
+        factor_kernel,
+        out_shape=(
+            jax.ShapeDtypeStruct((256, 256), F32),
+            jax.ShapeDtypeStruct(left_out.shape, F32),
+            jax.ShapeDtypeStruct((right_out.shape[1], 256), F32),
+        ),
+        in_specs=[vmem_spec] * 3,
+        out_specs=(vmem_spec, hbm_spec, hbm_spec),
+        scratch_shapes=[pltpu.VMEM((128, 256), F32), pltpu.SemaphoreType.DMA((3,))],
+        compiler_params=pltpu.CompilerParams(vmem_limit_bytes=8 << 20),
+        name="factor_and_place",
+    )(gram, left_out, right_out)
 
 
 def per_device(left_core, right_core, sizes):
@@ -329,7 +341,8 @@
     right = right_core.reshape(rank_mid * points, rank_right)
     root = float(rank_left * total_points) ** 0.5
     norm = 1.0 / (RK * total_points)
-    left_out, right_out, factor = whole(left, right, sizes, points, root, norm)
+    left_out, right_out, gram = whole(left, right, sizes, points, root, norm)
+    factor, left_out, right_out = factor_and_place(gram, left_out, right_out)
     return (
         left_out.reshape(rank_left, points, RK),
         right_out.reshape(RK, points, rank_right),

time: 71.5 us -> 66.8 us (0.934)
  local copies, waits for them, and re-layouts: 5.22 us -> 0 us
    pallas_call x0 -> x1, Pallas kernels: none -> 10.2 us  [factor_and_place(): pl.pallas_call(factor_kernel, out_shape=(jax.ShapeDtypeStruct((256, 256),...]
    pallas_call x1, Pallas kernels: 65.5 us -> 55.7 us  [whole(): pl.pallas_call(functools.partial(whole_kernel, sizes, points, root, norm)...]
    unnamed x7 -> x0, local copies, waits for them, and re-layouts: 5.22 us -> none
where the time goes in v3:
time: 66.8 us; the launch traced here: 66.7 us
  Pallas kernels  65.9 us (99%)
  between operations  0.8 us (1%)
    pallas_call x1, Pallas kernels, whole(): pl.pallas_call(functools.partial(whole_kernel, sizes, points, root, norm)...  55.7 us
    pallas_call x1, Pallas kernels, factor_and_place(): pl.pallas_call(factor_kernel, out_shape=(jax.ShapeDtypeStruct((256, 256),...  10.2 us

profile of v3, /device:TPU:1, one launch (start us, length us, event | category | flops | bytes accessed | tf_op | source)
XLA Modules:
  0.0 66.7 jit_solution(6976937329004504711)
XLA Ops:
  0.6 55.7 %whole.1 = (f32[4096,128]{1,0:T(8,128)S(1)}, f32[2,2048,128]{2,1,0:T(8,128)S(1)}, f32[32,2,8,128]{3,2,1,0:T(8,128)S(1)}) custom-call(f32[4096,256]{1,0:T(8,128)} %bitcast.4, f32[4096,256]{1,0:T(8,128)} %bitcast.5), custom_call_target="tpu_custom_call" | custom-call | tf_op jit(solution)/shard_map/whole/pallas_call | solution.py:261
  56.3 10.2 %factor_and_place.1 = (f32[256,256]{1,0:T(8,128)}, f32[4096,128]{1,0:T(8,128)}, f32[2048,256]{1,0:T(8,128)}) custom-call(f32[32,2,8,128]{3,2,1,0:T(8,128)S(1)} %get-tuple-element.9.g_ref, f32[4096,128]{1,0:T(8,128)S(1)} %get-tuple-element.10.lo_in, f32[2,2048,128]{2,1,0:T(8,128)S(1)} %get-tuple-element.11.ro_in), custom_call_target="tpu_custom_call" | custom-call | tf_op jit(solution)/shard_map/factor_and_place/pallas_call | solution.py:321

commit v4 on v3

--- a/solution.py
+++ b/solution.py
@@ -11,6 +11,7 @@
 F32 = jnp.float32
 BF16 = jnp.bfloat16
 MESH = pl.DeviceIdType.MESH
+AXES = ("gx", "gy", "gz")
 
 
 def split(x):
@@ -26,82 +27,69 @@
     return lax.dot_general(a, b, (((0,), (0,)), ((), ())), preferred_element_type=F32)
 
 
+def near(d, n):
+    return min(d, n - d)
+
+
+def plane(sizes):
+    nx, ny, _ = sizes
+    chips = nx // 2
+    offsets = [(dx, dc, dy) for dx in range(chips) for dc in range(2) for dy in range(ny)][1:]
+    offsets.sort(key=lambda o: -near(o[0], chips) - near(o[2], ny))
+    gx, gy, gz = (lax.axis_index(a) for a in AXES)
+    x, core = lax.div(gx, 2), lax.rem(gx, 2)
+    xs = {(dx, dc): lax.rem(x + dx, chips) * 2 + lax.rem(core + dc, 2) for dx in range(chips) for dc in range(2)}
+    ys = [lax.rem(gy + dy, ny) for dy in range(ny)]
+    return [(xs[dx, dc] * ny + ys[dy], (xs[dx, dc], ys[dy], gz)) for dx, dc, dy in offsets]
+
+
+def line(sizes):
+    nz = sizes[2]
+    gx, gy, gz = (lax.axis_index(a) for a in AXES)
+    return [(gx, gy, lax.rem(gz + d, nz)) for d in sorted(range(1, nz), key=lambda d: -near(d, nz))]
+
+
 def exchange(sizes, src, out, rx, rz, sems, meanwhile):
     nx, ny, nz = sizes
-    gx, gy, gz = lax.axis_index("gx"), lax.axis_index("gy"), lax.axis_index("gz")
     n = nx * ny
-    me = gx * ny + gy
-
-    def scatter(s):
-        k, dev = plane(sizes, s)
+    gz = lax.axis_index("gz")
+    me = lax.axis_index("gx") * ny + lax.axis_index("gy")
+    in_plane, in_line = plane(sizes), line(sizes)
+
+    def copy(a, b, phase, dev):
         return pltpu.make_async_remote_copy(
-            src.at[k], rx.at[s], sems.at[0, s], sems.at[1, s], device_id=dev, device_id_type=MESH
+            a, b, sems.at[2 * phase], sems.at[2 * phase + 1], device_id=dev, device_id_type=MESH
         )
 
-    def across(s):
-        return pltpu.make_async_remote_copy(
-            rz.at[gz], rz.at[gz], sems.at[2, s], sems.at[3, s], device_id=line(sizes, s), device_id_type=MESH
-        )
-
-    def gather(s):
-        return pltpu.make_async_remote_copy(
-            out.at[me], out.at[me], sems.at[4, s], sems.at[5, s], device_id=plane(sizes, s)[1], device_id_type=MESH
-        )
-
-    @pl.loop(1, n)
-    def _(s):
-        scatter(s).start()
-
+    for s, (k, dev) in enumerate(in_plane):
+        copy(src.at[k], rx.at[s], 0, dev).start()
     meanwhile()
-
-    def take(s, acc):
-        scatter(s).wait_recv()
-        return acc + rx[s]
-
-    rz[gz] = lax.fori_loop(1, n, take, src[me])
-
-    @pl.loop(1, nz)
-    def _(s):
-        across(s).start()
-
-    @pl.loop(1, nz)
-    def _(s):
-        across(s).wait_recv()
-
+    scatter = copy(rx, rx, 0, in_plane[0][1])
+    scatter.wait_recv()
+    total = src[me]
+    for s in range(n - 1):
+        total = total + rx[s]
+    rz[gz] = total
+    for dev in in_line:
+        copy(rz.at[gz], rz.at[gz], 1, dev).start()
+    rest = rz.at[pl.ds(0, nz - 1)]
+    across = copy(rest, rest, 1, in_line[0])
+    across.wait_recv()
     total = rz[0]
     for z in range(1, nz):
         total = total + rz[z]
     out[me] = total
-
-    @pl.loop(1, n)
-    def _(s):
-        gather(s).start()
-
-    @pl.loop(1, n)
-    def _(s):
-        gather(s).wait_recv()
+    for _, dev in in_plane:
+        copy(out.at[me], out.at[me], 2, dev).start()
+    rest = out.at[pl.ds(0, n - 1)]
+    gather = copy(rest, rest, 2, in_plane[0][1])
+    gather.wait_recv()
 
     def finish():
-        @pl.loop(1, n)
-        def _(s):
-            scatter(s).wait_send()
-            gather(s).wait_send()
-
-        @pl.loop(1, nz)
-        def _(s):
-            across(s).wait_send()
+        for waited in (scatter, across, gather):
+            waited.wait_send()
 
     return finish
-
-
-def plane(sizes, step):
-    n = sizes[0] * sizes[1]
-    k = lax.rem(lax.axis_index("gx") * sizes[1] + lax.axis_index("gy") + step, n)
-    return k, (lax.div(k, sizes[1]), lax.rem(k, sizes[1]), lax.axis_index("gz"))
-
-
-def line(sizes, step):
-    return (lax.axis_index("gx"), lax.axis_index("gy"), lax.rem(lax.axis_index("gz") + step, sizes[2]))
 
 
 def eliminate(work, tiles):
@@ -181,13 +169,8 @@
 
     barrier = pltpu.get_barrier_semaphore()
 
-    @pl.loop(1, nx * ny)
-    def _(s):
-        pl.semaphore_signal(barrier, inc=1, device_id=plane(sizes, s)[1], device_id_type=MESH)
-
-    @pl.loop(1, nz)
-    def _(s):
-        pl.semaphore_signal(barrier, inc=1, device_id=line(sizes, s), device_id_type=MESH)
+    for dev in [dev for _, dev in plane(sizes)] + line(sizes):
+        pl.semaphore_signal(barrier, inc=1, device_id=dev, device_id_type=MESH)
 
     gram = jnp.zeros((RK, 256), F32)
     for get, at in zip(get_left, spans):
@@ -275,14 +258,14 @@
             pltpu.VMEM((128, 384), F32),
             pltpu.VMEM((32, 1, 8, 128), F32),
             pltpu.VMEM((32, 1, 8, 128), F32),
-            pltpu.VMEM((n, 1, 8, 128), F32),
+            pltpu.VMEM((n - 1, 1, 8, 128), F32),
             pltpu.VMEM((nz, 1, 8, 128), F32),
             pltpu.VMEM((32, 2, 8, 128), F32),
             pltpu.VMEM((32, 2, 8, 128), F32),
-            pltpu.VMEM((n, 2, 8, 128), F32),
+            pltpu.VMEM((n - 1, 2, 8, 128), F32),
             pltpu.VMEM((nz, 2, 8, 128), F32),
-            pltpu.SemaphoreType.DMA((6, n)),
-            pltpu.SemaphoreType.DMA((6, n)),
+            pltpu.SemaphoreType.DMA((6,)),
+            pltpu.SemaphoreType.DMA((6,)),
             pltpu.SemaphoreType.DMA((6,)),
         ],
         compiler_params=pltpu.CompilerParams(

time: 66.8 us -> 60.2 us (0.901)
  Pallas kernels: 65.9 us -> 59.3 us
    pallas_call x1, Pallas kernels: 55.7 us -> 48.9 us  [whole(): pl.pallas_call(functools.partial(whole_kernel, sizes, points, root, norm)...]
where the time goes in v4:
time: 60.2 us; the launch traced here: 60.1 us
  Pallas kernels  59.3 us (99%)
  between operations  0.8 us (1%)
    pallas_call x1, Pallas kernels, whole(): pl.pallas_call(functools.partial(whole_kernel, sizes, points, root, norm)...  48.9 us
    pallas_call x1, Pallas kernels, factor_and_place(): pl.pallas_call(factor_kernel, out_shape=(jax.ShapeDtypeStruct((256, 256),...  10.4 us

profile of v4, /device:TPU:1, one launch (start us, length us, event | category | flops | bytes accessed | tf_op | source)
XLA Modules:
  0.0 60.1 jit_solution(18075243115899558931)
XLA Ops:
  0.6 48.9 %whole.1 = (f32[4096,128]{1,0:T(8,128)S(1)}, f32[2,2048,128]{2,1,0:T(8,128)S(1)}, f32[32,2,8,128]{3,2,1,0:T(8,128)S(1)}) custom-call(f32[4096,256]{1,0:T(8,128)} %bitcast.4, f32[4096,256]{1,0:T(8,128)} %bitcast.5), custom_call_target="tpu_custom_call" | custom-call | tf_op jit(solution)/shard_map/whole/pallas_call | solution.py:244
  49.6 10.4 %factor_and_place.1 = (f32[256,256]{1,0:T(8,128)}, f32[4096,128]{1,0:T(8,128)}, f32[2048,256]{1,0:T(8,128)}) custom-call(f32[32,2,8,128]{3,2,1,0:T(8,128)S(1)} %get-tuple-element.9.g_ref, f32[4096,128]{1,0:T(8,128)S(1)} %get-tuple-element.10.lo_in, f32[2,2048,128]{2,1,0:T(8,128)S(1)} %get-tuple-element.11.ro_in), custom_call_target="tpu_custom_call" | custom-call | tf_op jit(solution)/shard_map/factor_and_place/pallas_call | solution.py:304

commit v5 on v4

--- a/solution.py
+++ b/solution.py
@@ -49,7 +49,7 @@
     return [(gx, gy, lax.rem(gz + d, nz)) for d in sorted(range(1, nz), key=lambda d: -near(d, nz))]
 
 
-def exchange(sizes, src, out, rx, rz, sems, meanwhile):
+def exchange(sizes, src, out, rx, rz, sems, first=None, last=None):
     nx, ny, nz = sizes
     n = nx * ny
     gz = lax.axis_index("gz")
@@ -63,7 +63,8 @@
 
     for s, (k, dev) in enumerate(in_plane):
         copy(src.at[k], rx.at[s], 0, dev).start()
-    meanwhile()
+    if first is not None:
+        first()
     scatter = copy(rx, rx, 0, in_plane[0][1])
     scatter.wait_recv()
     total = src[me]
@@ -83,6 +84,8 @@
         copy(out.at[me], out.at[me], 2, dev).start()
     rest = out.at[pl.ds(0, n - 1)]
     gather = copy(rest, rest, 2, in_plane[0][1])
+    if last is not None:
+        last()
     gather.wait_recv()
 
     def finish():
@@ -94,17 +97,24 @@
 
 def eliminate(work, tiles):
     shape = (8, 128)
+    sub = lax.broadcasted_iota(jnp.int32, shape, 0)
+
+    def lane(x, c):
+        return jnp.take_along_axis(x, jnp.full(shape, c, jnp.int32), axis=1)
+
+    def row(x, i):
+        return jnp.take_along_axis(x, jnp.full(shape, i, jnp.int32), axis=0)
+
     for b in range(16):
         r0 = 8 * b
         rows8 = pl.ds(r0, 8)
         panel = [work[rows8, 128 * t : 128 * t + 128] for t in range(tiles)]
 
         def lanes(x):
-            return [jnp.broadcast_to(x[:, r0 + k : r0 + k + 1], shape) for k in range(8)]
+            return [lane(x, r0 + k) for k in range(8)]
 
         cols = lanes(panel[0])
-        e = [[jnp.broadcast_to(cols[k][i : i + 1, :], shape) if k <= i else None for k in range(8)] for i in range(8)]
-        rows = [[jnp.broadcast_to(p[i : i + 1, :], shape) for i in range(8)] for p in panel]
+        e = [[row(cols[k], i) if k <= i else None for k in range(8)] for i in range(8)]
         scale, mult = [], []
         for i in range(8):
             rs = lax.rsqrt(e[i][i])
@@ -117,7 +127,7 @@
             scale.append(rs)
             mult.append(l)
 
-        def apply(v):
+        def forward(v):
             v = list(v)
             for i in range(8):
                 v[i] = v[i] * scale[i]
@@ -125,20 +135,33 @@
                     v[k] = v[k] - mult[i][k] * v[i]
             return v
 
-        rows = [apply(r) for r in rows]
-        sub = lax.broadcasted_iota(jnp.int32, shape, 0)
+        def backward(v):
+            v = list(v)
+            for i in range(7, -1, -1):
+                v[i] = v[i] * scale[i]
+                for k in range(i):
+                    v[k] = v[k] - mult[k][i] * v[i]
+            return v
+
+        rows = [forward([row(p, i) for i in range(8)]) for p in panel]
         for t in range(tiles):
             out = rows[t][0]
             for i in range(1, 8):
                 out = jnp.where(sub == i, rows[t][i], out)
             work[rows8, 128 * t : 128 * t + 128] = out
+        solved = [backward(r) for r in rows] if tiles > 1 else None
         for m in range(b + 1, 16):
             m8 = pl.ds(8 * m, 8)
-            cm = apply(lanes(work[m8, 0:128]))
+            left = lanes(work[m8, 0:128])
+            right = rows
+            if m == b + 1 or solved is None:
+                left = forward(left)
+            else:
+                right = solved
             for t in range(tiles):
                 v = work[m8, 128 * t : 128 * t + 128]
                 for k in range(8):
-                    v = v - cm[k] * rows[t][k]
+                    v = v - left[k] * right[t][k]
                 work[m8, 128 * t : 128 * t + 128] = v
 
 
@@ -153,18 +176,17 @@
 
 
 def whole_kernel(sizes, points, root, norm, left_hbm, right_hbm, lout, rout, g2_ref,
-                 lbuf, rbuf, r_hi, r_lo, work, src1, sum1, rx1, rz1, src2, sum2, rx2, rz2,
+                 lbuf, rbuf, r_hi, r_lo, o_hi, o_lo, work, src1, sum1, rx1, rz1, src2, sum2, rx2, rz2,
                  sems1, sems2, sem):
     nx, ny, nz = sizes
     rows = lbuf.shape[0]
-    chunks = 4
-    size = rows // chunks
-    spans = [pl.ds(c * size, size) for c in range(chunks)]
+    bounds = [0, rows // 8, rows * 5 // 16, rows * 19 // 32, rows]
+    spans = [pl.ds(lo, hi - lo) for lo, hi in zip(bounds, bounds[1:])]
     get_left = [pltpu.make_async_copy(left_hbm.at[at, :], lbuf.at[at, :], sem.at[c]) for c, at in enumerate(spans)]
     get_right = [
         pltpu.make_async_copy(right_hbm.at[:, 128 * h : 128 * h + 128], rbuf.at[h], sem.at[4 + h]) for h in range(2)
     ]
-    for get in get_left + get_right:
+    for get in get_left:
         get.start()
 
     barrier = pltpu.get_barrier_semaphore()
@@ -178,6 +200,8 @@
         hi, lo = split(lbuf[at, :])
         main = mm_tn(jnp.concatenate([hi[:, :RK], lo[:, :RK]], axis=1), hi)
         gram = gram + (main[:RK] + (main[RK:] + mm_tn(hi[:, :RK], lo)))
+    for get in get_right:
+        get.start()
     for half in range(2):
         src1[half * 16 : half * 16 + 16] = gram[:, half * RK : half * RK + RK].reshape(16, 1, 8, 128)
 
@@ -193,7 +217,7 @@
                 r_hi[p, :, 128 * h : 128 * h + 128] = hi
                 r_lo[p, :, 128 * h : 128 * h + 128] = lo
 
-    finish1 = exchange(sizes, src1, sum1, rx1, rz1, sems1, prepare_right)
+    finish1 = exchange(sizes, src1, sum1, rx1, rz1, sems1, last=prepare_right)
 
     work[:, 0:128] = sum1[0:16].reshape(128, 128)
     work[:, 128:256] = sum1[16:32].reshape(128, 128)
@@ -202,20 +226,15 @@
     upper = jnp.concatenate([jnp.where(upper_mask(), work[:, 0:128], 0.0), work[:, 128:256]], axis=1)
     up_hi, up_lo = split(upper)
     up_both = jnp.concatenate([up_hi, up_lo], axis=0)
-    g_main = jnp.zeros((256, 256), F32)
-    g_cross = jnp.zeros((256, 256), F32)
-    for pair in range(points // 2):
-        both = []
-        for p in (2 * pair, 2 * pair + 1):
-            main = mm(up_both, r_hi[p])
-            o = main[:128] + (main[128:] + mm(up_hi, r_lo[p]))
-            for h in range(2):
-                rout[h, pl.ds(p, 128, stride=points), :] = o[:, 128 * h : 128 * h + 128]
-            both.append(o)
-        o_hi, o_lo = split(jnp.concatenate(both, axis=0))
-        g_main = g_main + mm_tn(o_hi, o_hi)
-        g_cross = g_cross + mm_tn(o_hi, o_lo)
-    gram = (g_main + (g_cross + g_cross.T)) * norm
+    for p in range(points):
+        main = mm(up_both, r_hi[p])
+        o = main[:128] + (main[128:] + mm(up_hi, r_lo[p]))
+        for h in range(2):
+            rout[h, pl.ds(p, 128, stride=points), :] = o[:, 128 * h : 128 * h + 128]
+        at = pl.ds(128 * p, 128)
+        o_hi[at, :], o_lo[at, :] = split(o)
+    cross = mm_tn(o_hi[...], o_lo[...])
+    gram = (mm_tn(o_hi[...], o_hi[...]) + (cross + cross.T)) * norm
     for half in range(2):
         src2[:, half] = gram[:, 128 * half : 128 * half + 128].reshape(32, 8, 128)
 
@@ -229,7 +248,7 @@
             y = mm(jnp.concatenate([x_hi, x_lo], axis=1), weights)
             lout[at, :] = y[:, :128] + y[:, 128:]
 
-    finish2 = exchange(sizes, src2, sum2, rx2, rz2, sems2, make_left)
+    finish2 = exchange(sizes, src2, sum2, rx2, rz2, sems2, first=make_left)
 
     g2_ref[...] = sum2[...]
     finish1()
@@ -255,6 +274,8 @@
             pltpu.VMEM((2, right.shape[0], 128), F32),
             pltpu.VMEM((points, 256, 256), BF16),
             pltpu.VMEM((points, 256, 256), BF16),
+            pltpu.VMEM((out_rows, 256), BF16),
+            pltpu.VMEM((out_rows, 256), BF16),
             pltpu.VMEM((128, 384), F32),
             pltpu.VMEM((32, 1, 8, 128), F32),
             pltpu.VMEM((32, 1, 8, 128), F32),

time: 60.2 us -> 54.2 us (0.900)
  Pallas kernels: 59.3 us -> 53.3 us
    pallas_call x1, Pallas kernels: 10.4 us -> 6.73 us  [factor_and_place(): pl.pallas_call(factor_kernel, out_shape=(jax.ShapeDtypeStruct((256, 256),...]
    pallas_call x1, Pallas kernels: 48.9 us -> 46.6 us  [whole(): pl.pallas_call(functools.partial(whole_kernel, sizes, points, root, norm)...]
where the time goes in v5:
time: 54.2 us; the launch traced here: 54.1 us
  Pallas kernels  53.3 us (98%)
  between operations  0.8 us (1%)
    pallas_call x1, Pallas kernels, whole(): pl.pallas_call(functools.partial(whole_kernel, sizes, points, root, norm)...  46.6 us
    pallas_call x1, Pallas kernels, factor_and_place(): pl.pallas_call(factor_kernel, out_shape=(jax.ShapeDtypeStruct((256, 256),...  6.73 us

profile of v5, /device:TPU:1, one launch (start us, length us, event | category | flops | bytes accessed | tf_op | source)
XLA Modules:
  0.0 54.1 jit_solution(2549160428504617821)
XLA Ops:
  0.6 46.6 %whole.1 = (f32[4096,128]{1,0:T(8,128)S(1)}, f32[2,2048,128]{2,1,0:T(8,128)S(1)}, f32[32,2,8,128]{3,2,1,0:T(8,128)S(1)}) custom-call(f32[4096,256]{1,0:T(8,128)} %bitcast.4, f32[4096,256]{1,0:T(8,128)} %bitcast.5), custom_call_target="tpu_custom_call" | custom-call | tf_op jit(solution)/shard_map/whole/pallas_call | solution.py:263
  47.3 6.7 %factor_and_place.1 = (f32[256,256]{1,0:T(8,128)}, f32[4096,128]{1,0:T(8,128)}, f32[2048,256]{1,0:T(8,128)}) custom-call(f32[32,2,8,128]{3,2,1,0:T(8,128)S(1)} %get-tuple-element.9.g_ref, f32[4096,128]{1,0:T(8,128)S(1)} %get-tuple-element.10.lo_in, f32[2,2048,128]{2,1,0:T(8,128)S(1)} %get-tuple-element.11.ro_in), custom_call_target="tpu_custom_call" | custom-call | tf_op jit(solution)/shard_map/factor_and_place/pallas_call | solution.py:325

commit v6 on v5

--- a/solution.py
+++ b/solution.py
@@ -34,13 +34,13 @@
 def plane(sizes):
     nx, ny, _ = sizes
     chips = nx // 2
-    offsets = [(dx, dc, dy) for dx in range(chips) for dc in range(2) for dy in range(ny)][1:]
-    offsets.sort(key=lambda o: -near(o[0], chips) - near(o[2], ny))
+    offsets = [(dx, dy) for dx in range(chips) for dy in range(ny)][1:]
+    offsets.sort(key=lambda o: -near(o[0], chips) - near(o[1], ny))
     gx, gy, gz = (lax.axis_index(a) for a in AXES)
     x, core = lax.div(gx, 2), lax.rem(gx, 2)
-    xs = {(dx, dc): lax.rem(x + dx, chips) * 2 + lax.rem(core + dc, 2) for dx in range(chips) for dc in range(2)}
+    xs = [lax.rem(x + dx, chips) for dx in range(chips)]
     ys = [lax.rem(gy + dy, ny) for dy in range(ny)]
-    return [(xs[dx, dc] * ny + ys[dy], (xs[dx, dc], ys[dy], gz)) for dx, dc, dy in offsets]
+    return [(xs[dx] * ny + ys[dy], (xs[dx] * 2 + core, ys[dy], gz)) for dx, dy in offsets]
 
 
 def line(sizes):
@@ -49,47 +49,56 @@
     return [(gx, gy, lax.rem(gz + d, nz)) for d in sorted(range(1, nz), key=lambda d: -near(d, nz))]
 
 
-def exchange(sizes, src, out, rx, rz, sems, first=None, last=None):
+def partner():
+    gx, gy, gz = (lax.axis_index(a) for a in AXES)
+    return (gx + 1 - 2 * lax.rem(gx, 2), gy, gz)
+
+
+def exchange(sizes, src, out, rc, part, rx, rz, sems, hooks):
     nx, ny, nz = sizes
-    n = nx * ny
-    gz = lax.axis_index("gz")
-    me = lax.axis_index("gx") * ny + lax.axis_index("gy")
-    in_plane, in_line = plane(sizes), line(sizes)
+    n = nx // 2 * ny
+    gx, gz = lax.axis_index("gx"), lax.axis_index("gz")
+    core = lax.rem(gx, 2)
+    me = lax.div(gx, 2) * ny + lax.axis_index("gy")
+    other, in_plane, in_line = partner(), plane(sizes), line(sizes)
+    waits = []
 
     def copy(a, b, phase, dev):
         return pltpu.make_async_remote_copy(
             a, b, sems.at[2 * phase], sems.at[2 * phase + 1], device_id=dev, device_id_type=MESH
         )
 
+    def receive(ref, phase, dev):
+        if phase in hooks:
+            hooks[phase]()
+        waits.append(copy(ref, ref, phase, dev))
+        waits[-1].wait_recv()
+
+    copy(src.at[1 - core], rc, 0, other).start()
+    receive(rc, 0, other)
+    part[...] = src[core] + rc[...]
     for s, (k, dev) in enumerate(in_plane):
-        copy(src.at[k], rx.at[s], 0, dev).start()
-    if first is not None:
-        first()
-    scatter = copy(rx, rx, 0, in_plane[0][1])
-    scatter.wait_recv()
-    total = src[me]
+        copy(part.at[k], rx.at[s], 1, dev).start()
+    receive(rx, 1, in_plane[0][1])
+    total = part[me]
     for s in range(n - 1):
         total = total + rx[s]
     rz[gz] = total
     for dev in in_line:
-        copy(rz.at[gz], rz.at[gz], 1, dev).start()
-    rest = rz.at[pl.ds(0, nz - 1)]
-    across = copy(rest, rest, 1, in_line[0])
-    across.wait_recv()
+        copy(rz.at[gz], rz.at[gz], 2, dev).start()
+    receive(rz.at[pl.ds(0, nz - 1)], 2, in_line[0])
     total = rz[0]
     for z in range(1, nz):
         total = total + rz[z]
-    out[me] = total
+    out[core, me] = total
     for _, dev in in_plane:
-        copy(out.at[me], out.at[me], 2, dev).start()
-    rest = out.at[pl.ds(0, n - 1)]
-    gather = copy(rest, rest, 2, in_plane[0][1])
-    if last is not None:
-        last()
-    gather.wait_recv()
+        copy(out.at[core, me], out.at[core, me], 3, dev).start()
+    receive(out.at[0, pl.ds(0, n - 1)], 3, in_plane[0][1])
+    copy(out.at[core], out.at[core], 4, other).start()
+    receive(out.at[0], 4, other)
 
     def finish():
-        for waited in (scatter, across, gather):
+        for waited in waits:
             waited.wait_send()
 
     return finish
@@ -176,7 +185,8 @@
 
 
 def whole_kernel(sizes, points, root, norm, left_hbm, right_hbm, lout, rout, g2_ref,
-                 lbuf, rbuf, r_hi, r_lo, o_hi, o_lo, work, src1, sum1, rx1, rz1, src2, sum2, rx2, rz2,
+                 lbuf, rbuf, r_hi, r_lo, o_hi, o_lo, o_all, work,
+                 src1, sum1, rc1, part1, rx1, rz1, src2, sum2, rc2, part2, rx2, rz2,
                  sems1, sems2, sem):
     nx, ny, nz = sizes
     rows = lbuf.shape[0]
@@ -191,7 +201,7 @@
 
     barrier = pltpu.get_barrier_semaphore()
 
-    for dev in [dev for _, dev in plane(sizes)] + line(sizes):
+    for dev in [partner()] + [dev for _, dev in plane(sizes)] + line(sizes):
         pl.semaphore_signal(barrier, inc=1, device_id=dev, device_id_type=MESH)
 
     gram = jnp.zeros((RK, 256), F32)
@@ -203,9 +213,9 @@
     for get in get_right:
         get.start()
     for half in range(2):
-        src1[half * 16 : half * 16 + 16] = gram[:, half * RK : half * RK + RK].reshape(16, 1, 8, 128)
-
-    pl.semaphore_wait(barrier, nx * ny - 1 + nz - 1)
+        src1[half] = gram[:, half * RK : half * RK + RK].reshape(16, 1, 8, 128)
+
+    pl.semaphore_wait(barrier, nx // 2 * ny + nz - 1)
 
     def prepare_right():
         for get in get_right:
@@ -217,29 +227,37 @@
                 r_hi[p, :, 128 * h : 128 * h + 128] = hi
                 r_lo[p, :, 128 * h : 128 * h + 128] = lo
 
-    finish1 = exchange(sizes, src1, sum1, rx1, rz1, sems1, last=prepare_right)
-
-    work[:, 0:128] = sum1[0:16].reshape(128, 128)
-    work[:, 128:256] = sum1[16:32].reshape(128, 128)
-    work[:, 256:384] = identity()
-    eliminate(work, 3)
+    finish1 = exchange(sizes, src1, sum1, rc1, part1, rx1, rz1, sems1, {3: prepare_right})
+
+    work[:, 0:128] = sum1[0].reshape(128, 128)
+    work[:, 128:256] = sum1[1].reshape(128, 128)
+    eliminate(work, 2)
     upper = jnp.concatenate([jnp.where(upper_mask(), work[:, 0:128], 0.0), work[:, 128:256]], axis=1)
     up_hi, up_lo = split(upper)
     up_both = jnp.concatenate([up_hi, up_lo], axis=0)
     for p in range(points):
         main = mm(up_both, r_hi[p])
         o = main[:128] + (main[128:] + mm(up_hi, r_lo[p]))
-        for h in range(2):
-            rout[h, pl.ds(p, 128, stride=points), :] = o[:, 128 * h : 128 * h + 128]
         at = pl.ds(128 * p, 128)
+        o_all[at, :] = o
         o_hi[at, :], o_lo[at, :] = split(o)
     cross = mm_tn(o_hi[...], o_lo[...])
     gram = (mm_tn(o_hi[...], o_hi[...]) + (cross + cross.T)) * norm
     for half in range(2):
-        src2[:, half] = gram[:, 128 * half : 128 * half + 128].reshape(32, 8, 128)
+        src2[:, :, half] = gram[:, 128 * half : 128 * half + 128].reshape(2, 16, 8, 128)
+
+    def invert():
+        work[:, 0:128] = sum1[0].reshape(128, 128)
+        work[:, 128:256] = identity()
+        eliminate(work, 2)
+
+    def place_right():
+        for p in range(points):
+            for h in range(2):
+                rout[h, pl.ds(p, 128, stride=points), :] = o_all[128 * p : 128 * p + 128, 128 * h : 128 * h + 128]
 
     def make_left():
-        w_hi, w_lo = split(work[:, 256:384].T * root)
+        w_hi, w_lo = split(work[:, 128:256].T * root)
         weights = jnp.concatenate(
             [jnp.concatenate([w_hi, w_lo], axis=1), jnp.concatenate([w_hi, jnp.zeros_like(w_lo)], axis=1)], axis=0
         )
@@ -248,8 +266,8 @@
             y = mm(jnp.concatenate([x_hi, x_lo], axis=1), weights)
             lout[at, :] = y[:, :128] + y[:, 128:]
 
-    finish2 = exchange(sizes, src2, sum2, rx2, rz2, sems2, first=make_left)
-
+    hooks = {1: invert, 2: place_right, 3: make_left}
+    finish2 = exchange(sizes, src2, sum2, rc2, part2, rx2, rz2, sems2, hooks)
     g2_ref[...] = sum2[...]
     finish1()
     finish2()
@@ -258,14 +276,14 @@
 def whole(left, right, sizes, points, root, norm):
     rows = left.shape[0]
     out_rows = RK * points
-    n, nz = sizes[0] * sizes[1], sizes[2]
+    n, nz = sizes[0] // 2 * sizes[1], sizes[2]
     any_spec = pl.BlockSpec(memory_space=pl.ANY)
     return pl.pallas_call(
         functools.partial(whole_kernel, sizes, points, root, norm),
         out_shape=(
             pltpu.VMEM((rows, RK), F32),
             pltpu.VMEM((2, out_rows, 128), F32),
-            pltpu.VMEM((32, 2, 8, 128), F32),
+            pltpu.VMEM((2, 16, 2, 8, 128), F32),
         ),
         in_specs=[any_spec, any_spec],
         out_specs=(pl.BlockSpec(memory_space=pltpu.VMEM),) * 3,
@@ -276,17 +294,15 @@
             pltpu.VMEM((points, 256, 256), BF16),
             pltpu.VMEM((out_rows, 256), BF16),
             pltpu.VMEM((out_rows, 256), BF16),
-            pltpu.VMEM((128, 384), F32),
-            pltpu.VMEM((32, 1, 8, 128), F32),
-            pltpu.VMEM((32, 1, 8, 128), F32),
-            pltpu.VMEM((n - 1, 1, 8, 128), F32),
-            pltpu.VMEM((nz, 1, 8, 128), F32),
-            pltpu.VMEM((32, 2, 8, 128), F32),
-            pltpu.VMEM((32, 2, 8, 128), F32),
-            pltpu.VMEM((n - 1, 2, 8, 128), F32),
-            pltpu.VMEM((nz, 2, 8, 128), F32),
-            pltpu.SemaphoreType.DMA((6,)),
-            pltpu.SemaphoreType.DMA((6,)),
+            pltpu.VMEM((out_rows, 256), F32),
+            pltpu.VMEM((128, 256), F32),
+            *[
+                pltpu.VMEM((*lead, tiles, 8, 128), F32)
+                for tiles in (1, 2)
+                for lead in ((2, n), (2, n), (n,), (n,), (n - 1,), (nz,))
+            ],
+            pltpu.SemaphoreType.DMA((10,)),
+            pltpu.SemaphoreType.DMA((10,)),
             pltpu.SemaphoreType.DMA((6,)),
         ],
         compiler_params=pltpu.CompilerParams(
@@ -302,8 +318,8 @@
         puts.append(pltpu.make_async_copy(ro_in.at[h], ro_out.at[:, 128 * h : 128 * h + 128], sem.at[h]))
     for put in puts:
         put.start()
-    work[:, 0:128] = g_ref[0:16, 0].reshape(128, 128)
-    work[:, 128:256] = g_ref[0:16, 1].reshape(128, 128)
+    work[:, 0:128] = g_ref[0, :, 0].reshape(128, 128)
+    work[:, 128:256] = g_ref[0, :, 1].reshape(128, 128)
     eliminate(work, 2)
     right = work[:, 128:256]
     f_ref[0:128, 0:128] = jnp.where(upper_mask(), work[:, 0:128], 0.0)
@@ -311,7 +327,7 @@
     update = lax.dot_general(
         right, right, (((0,), (0,)), ((), ())), precision=lax.Precision.HIGHEST, preferred_element_type=F32
     )
-    work[:, 0:128] = g_ref[16:32, 1].reshape(128, 128) - update
+    work[:, 0:128] = g_ref[1, :, 1].reshape(128, 128) - update
     eliminate(work, 1)
     f_ref[128:256, 0:128] = jnp.zeros((128, 128), F32)
     f_ref[128:256, 128:256] = jnp.where(upper_mask(), work[:, 0:128], 0.0)

time: 54.2 us -> 55.4 us (1.022)
  Pallas kernels: 53.3 us -> 54.5 us
    pallas_call x1, Pallas kernels: 46.6 us -> 47.9 us  [whole(): pl.pallas_call(functools.partial(whole_kernel, sizes, points, root, norm)...]
where the time goes in v6:
time: 55.4 us; the launch traced here: 55.3 us
  Pallas kernels  54.5 us (98%)
  between operations  0.8 us (1%)
    pallas_call x1, Pallas kernels, whole(): pl.pallas_call(functools.partial(whole_kernel, sizes, points, root, norm)...  47.9 us
    pallas_call x1, Pallas kernels, factor_and_place(): pl.pallas_call(factor_kernel, out_shape=(jax.ShapeDtypeStruct((256, 256),...  6.55 us

profile of v6, /device:TPU:1, one launch (start us, length us, event | category | flops | bytes accessed | tf_op | source)
XLA Modules:
  0.0 55.3 jit_solution(2337915285202139091)
XLA Ops:
  0.6 47.9 %whole.1 = (f32[4096,128]{1,0:T(8,128)S(1)}, f32[2,2048,128]{2,1,0:T(8,128)S(1)}, f32[2,16,2,8,128]{4,3,2,1,0:T(8,128)S(1)}) custom-call(f32[4096,256]{1,0:T(8,128)} %bitcast.4, f32[4096,256]{1,0:T(8,128)} %bitcast.5), custom_call_target="tpu_custom_call" | custom-call | tf_op jit(solution)/shard_map/whole/pallas_call | solution.py:281
  48.6 6.6 %factor_and_place.1 = (f32[256,256]{1,0:T(8,128)}, f32[4096,128]{1,0:T(8,128)}, f32[2048,256]{1,0:T(8,128)}) custom-call(f32[2,16,2,8,128]{4,3,2,1,0:T(8,128)S(1)} %get-tuple-element.9.g_ref, f32[4096,128]{1,0:T(8,128)S(1)} %get-tuple-element.10.lo_in, f32[2,2048,128]{2,1,0:T(8,128)S(1)} %get-tuple-element.11.ro_in), custom_call_target="tpu_custom_call" | custom-call | tf_op jit(solution)/shard_map/factor_and_place/pallas_call | solution.py:341

commit v7 on v5

--- a/solution.py
+++ b/solution.py
@@ -25,6 +25,10 @@
 
 def mm_tn(a, b):
     return lax.dot_general(a, b, (((0,), (0,)), ((), ())), preferred_element_type=F32)
+
+
+def nothing():
+    pass
 
 
 def near(d, n):
@@ -49,7 +53,7 @@
     return [(gx, gy, lax.rem(gz + d, nz)) for d in sorted(range(1, nz), key=lambda d: -near(d, nz))]
 
 
-def exchange(sizes, src, out, rx, rz, sems, first=None, last=None):
+def exchange(sizes, src, out, rx, rz, sems, hooks):
     nx, ny, nz = sizes
     n = nx * ny
     gz = lax.axis_index("gz")
@@ -63,8 +67,7 @@
 
     for s, (k, dev) in enumerate(in_plane):
         copy(src.at[k], rx.at[s], 0, dev).start()
-    if first is not None:
-        first()
+    hooks[0]()
     scatter = copy(rx, rx, 0, in_plane[0][1])
     scatter.wait_recv()
     total = src[me]
@@ -75,6 +78,7 @@
         copy(rz.at[gz], rz.at[gz], 1, dev).start()
     rest = rz.at[pl.ds(0, nz - 1)]
     across = copy(rest, rest, 1, in_line[0])
+    hooks[1]()
     across.wait_recv()
     total = rz[0]
     for z in range(1, nz):
@@ -84,8 +88,7 @@
         copy(out.at[me], out.at[me], 2, dev).start()
     rest = out.at[pl.ds(0, n - 1)]
     gather = copy(rest, rest, 2, in_plane[0][1])
-    if last is not None:
-        last()
+    hooks[2]()
     gather.wait_recv()
 
     def finish():
@@ -176,7 +179,7 @@
 
 
 def whole_kernel(sizes, points, root, norm, left_hbm, right_hbm, lout, rout, g2_ref,
-                 lbuf, rbuf, r_hi, r_lo, o_hi, o_lo, work, src1, sum1, rx1, rz1, src2, sum2, rx2, rz2,
+                 lbuf, rbuf, r_hi, r_lo, o_hi, o_lo, o_all, work, src1, sum1, rx1, rz1, src2, sum2, rx2, rz2,
                  sems1, sems2, sem):
     nx, ny, nz = sizes
     rows = lbuf.shape[0]
@@ -203,7 +206,7 @@
     for get in get_right:
         get.start()
     for half in range(2):
-        src1[half * 16 : half * 16 + 16] = gram[:, half * RK : half * RK + RK].reshape(16, 1, 8, 128)
+        src1[half * 16 : half * 16 + 16] = gram[:, half * RK : half * RK + RK].reshape(16, 8, 128)
 
     pl.semaphore_wait(barrier, nx * ny - 1 + nz - 1)
 
@@ -217,29 +220,39 @@
                 r_hi[p, :, 128 * h : 128 * h + 128] = hi
                 r_lo[p, :, 128 * h : 128 * h + 128] = lo
 
-    finish1 = exchange(sizes, src1, sum1, rx1, rz1, sems1, last=prepare_right)
+    finish1 = exchange(sizes, src1, sum1, rx1, rz1, sems1, (nothing, nothing, prepare_right))
 
     work[:, 0:128] = sum1[0:16].reshape(128, 128)
     work[:, 128:256] = sum1[16:32].reshape(128, 128)
-    work[:, 256:384] = identity()
-    eliminate(work, 3)
+    eliminate(work, 2)
     upper = jnp.concatenate([jnp.where(upper_mask(), work[:, 0:128], 0.0), work[:, 128:256]], axis=1)
     up_hi, up_lo = split(upper)
     up_both = jnp.concatenate([up_hi, up_lo], axis=0)
     for p in range(points):
         main = mm(up_both, r_hi[p])
         o = main[:128] + (main[128:] + mm(up_hi, r_lo[p]))
-        for h in range(2):
-            rout[h, pl.ds(p, 128, stride=points), :] = o[:, 128 * h : 128 * h + 128]
         at = pl.ds(128 * p, 128)
+        o_all[at, :] = o
         o_hi[at, :], o_lo[at, :] = split(o)
     cross = mm_tn(o_hi[...], o_lo[...])
     gram = (mm_tn(o_hi[...], o_hi[...]) + (cross + cross.T)) * norm
     for half in range(2):
-        src2[:, half] = gram[:, 128 * half : 128 * half + 128].reshape(32, 8, 128)
+        src2[16 * half : 16 * half + 16, 0:8] = gram[0:128, 128 * half : 128 * half + 128].reshape(16, 8, 128)
+    for k in range(32):
+        src2[k, 8:12] = gram[128 + 4 * k : 132 + 4 * k, 128:256]
+
+    def invert():
+        work[:, 0:128] = sum1[0:16].reshape(128, 128)
+        work[:, 128:256] = identity()
+        eliminate(work, 2)
+
+    def place_right():
+        for p in range(points):
+            for h in range(2):
+                rout[h, pl.ds(p, 128, stride=points), :] = o_all[128 * p : 128 * p + 128, 128 * h : 128 * h + 128]
 
     def make_left():
-        w_hi, w_lo = split(work[:, 256:384].T * root)
+        w_hi, w_lo = split(work[:, 128:256].T * root)
         weights = jnp.concatenate(
             [jnp.concatenate([w_hi, w_lo], axis=1), jnp.concatenate([w_hi, jnp.zeros_like(w_lo)], axis=1)], axis=0
         )
@@ -248,8 +261,7 @@
             y = mm(jnp.concatenate([x_hi, x_lo], axis=1), weights)
             lout[at, :] = y[:, :128] + y[:, 128:]
 
-    finish2 = exchange(sizes, src2, sum2, rx2, rz2, sems2, first=make_left)
-
+    finish2 = exchange(sizes, src2, sum2, rx2, rz2, sems2, (invert, place_right, make_left))
     g2_ref[...] = sum2[...]
     finish1()
     finish2()
@@ -265,7 +277,7 @@
         out_shape=(
             pltpu.VMEM((rows, RK), F32),
             pltpu.VMEM((2, out_rows, 128), F32),
-            pltpu.VMEM((32, 2, 8, 128), F32),
+            pltpu.VMEM((n, 12, 128), F32),
         ),
         in_specs=[any_spec, any_spec],
         out_specs=(pl.BlockSpec(memory_space=pltpu.VMEM),) * 3,
@@ -276,15 +288,9 @@
             pltpu.VMEM((points, 256, 256), BF16),
             pltpu.VMEM((out_rows, 256), BF16),
             pltpu.VMEM((out_rows, 256), BF16),
-            pltpu.VMEM((128, 384), F32),
-            pltpu.VMEM((32, 1, 8, 128), F32),
-            pltpu.VMEM((32, 1, 8, 128), F32),
-            pltpu.VMEM((n - 1, 1, 8, 128), F32),
-            pltpu.VMEM((nz, 1, 8, 128), F32),
-            pltpu.VMEM((32, 2, 8, 128), F32),
-            pltpu.VMEM((32, 2, 8, 128), F32),
-            pltpu.VMEM((n - 1, 2, 8, 128), F32),
-            pltpu.VMEM((nz, 2, 8, 128), F32),
+            pltpu.VMEM((out_rows, 256), F32),
+            pltpu.VMEM((128, 256), F32),
+            *[pltpu.VMEM((lead, high, 128), F32) for high in (8, 12) for lead in (n, n, n - 1, nz)],
             pltpu.SemaphoreType.DMA((6,)),
             pltpu.SemaphoreType.DMA((6,)),
             pltpu.SemaphoreType.DMA((6,)),
@@ -296,14 +302,16 @@
     )(left, right)
 
 
-def factor_kernel(g_ref, lo_in, ro_in, f_ref, lo_out, ro_out, work, sem):
+def factor_kernel(g_ref, lo_in, ro_in, f_ref, lo_out, ro_out, work, corner, sem):
     puts = [pltpu.make_async_copy(lo_in, lo_out, sem.at[2])]
     for h in range(2):
         puts.append(pltpu.make_async_copy(ro_in.at[h], ro_out.at[:, 128 * h : 128 * h + 128], sem.at[h]))
     for put in puts:
         put.start()
-    work[:, 0:128] = g_ref[0:16, 0].reshape(128, 128)
-    work[:, 128:256] = g_ref[0:16, 1].reshape(128, 128)
+    work[:, 0:128] = g_ref[0:16, 0:8].reshape(128, 128)
+    work[:, 128:256] = g_ref[16:32, 0:8].reshape(128, 128)
+    for k in range(32):
+        corner[4 * k : 4 * k + 4, :] = g_ref[k, 8:12]
     eliminate(work, 2)
     right = work[:, 128:256]
     f_ref[0:128, 0:128] = jnp.where(upper_mask(), work[:, 0:128], 0.0)
@@ -311,7 +319,7 @@
     update = lax.dot_general(
         right, right, (((0,), (0,)), ((), ())), precision=lax.Precision.HIGHEST, preferred_element_type=F32
     )
-    work[:, 0:128] = g_ref[16:32, 1].reshape(128, 128) - update
+    work[:, 0:128] = corner[...] - update
     eliminate(work, 1)
     f_ref[128:256, 0:128] = jnp.zeros((128, 128), F32)
     f_ref[128:256, 128:256] = jnp.where(upper_mask(), work[:, 0:128], 0.0)
@@ -331,7 +339,7 @@
         ),
         in_specs=[vmem_spec] * 3,
         out_specs=(vmem_spec, hbm_spec, hbm_spec),
-        scratch_shapes=[pltpu.VMEM((128, 256), F32), pltpu.SemaphoreType.DMA((3,))],
+        scratch_shapes=[pltpu.VMEM((128, 256), F32), pltpu.VMEM((128, 128), F32), pltpu.SemaphoreType.DMA((3,))],
         compiler_params=pltpu.CompilerParams(vmem_limit_bytes=8 << 20),
         name="factor_and_place",
     )(gram, left_out, right_out)

time: 54.2 us -> 52.6 us (0.970)
  Pallas kernels: 53.3 us -> 51.7 us
    pallas_call x1, Pallas kernels: 46.6 us -> 45.1 us  [whole(): pl.pallas_call(functools.partial(whole_kernel, sizes, points, root, norm)...]
where the time goes in v7:
time: 52.6 us; the launch traced here: 52.5 us
  Pallas kernels  51.7 us (98%)
  between operations  0.8 us (2%)
    pallas_call x1, Pallas kernels, whole(): pl.pallas_call(functools.partial(whole_kernel, sizes, points, root, norm)...  45.1 us
    pallas_call x1, Pallas kernels, factor_and_place(): pl.pallas_call(factor_kernel, out_shape=(jax.ShapeDtypeStruct((256, 256),...  6.55 us

profile of v7, /device:TPU:1, one launch (start us, length us, event | category | flops | bytes accessed | tf_op | source)
XLA Modules:
  0.0 52.5 jit_solution(12520887073751066390)
XLA Ops:
  0.6 45.1 %whole.1 = (f32[4096,128]{1,0:T(8,128)S(1)}, f32[2,2048,128]{2,1,0:T(8,128)S(1)}, f32[32,12,128]{2,1,0:T(8,128)S(1)}) custom-call(f32[4096,256]{1,0:T(8,128)} %bitcast.4, f32[4096,256]{1,0:T(8,128)} %bitcast.5), custom_call_target="tpu_custom_call" | custom-call | tf_op jit(solution)/shard_map/whole/pallas_call | solution.py:275
  45.7 6.6 %factor_and_place.1 = (f32[256,256]{1,0:T(8,128)}, f32[4096,128]{1,0:T(8,128)}, f32[2048,256]{1,0:T(8,128)}) custom-call(f32[32,12,128]{2,1,0:T(8,128)S(1)} %get-tuple-element.9.g_ref, f32[4096,128]{1,0:T(8,128)S(1)} %get-tuple-element.10.lo_in, f32[2,2048,128]{2,1,0:T(8,128)S(1)} %get-tuple-element.11.ro_in), custom_call_target="tpu_custom_call" | custom-call | tf_op jit(solution)/shard_map/factor_and_place/pallas_call | solution.py:333

commit v8 on v7

--- a/solution.py
+++ b/solution.py
@@ -179,7 +179,7 @@
 
 
 def whole_kernel(sizes, points, root, norm, left_hbm, right_hbm, lout, rout, g2_ref,
-                 lbuf, rbuf, r_hi, r_lo, o_hi, o_lo, o_all, work, src1, sum1, rx1, rz1, src2, sum2, rx2, rz2,
+                 lbuf, rbuf, r_hi, r_lo, o_hi, o_lo, o_all, work, src1, sum1, rx1, rz1, src2, rx2, rz2,
                  sems1, sems2, sem):
     nx, ny, nz = sizes
     rows = lbuf.shape[0]
@@ -201,8 +201,9 @@
     for get, at in zip(get_left, spans):
         get.wait()
         hi, lo = split(lbuf[at, :])
-        main = mm_tn(jnp.concatenate([hi[:, :RK], lo[:, :RK]], axis=1), hi)
-        gram = gram + (main[:RK] + (main[RK:] + mm_tn(hi[:, :RK], lo)))
+        both = jnp.concatenate([hi[:, :RK], lo[:, :RK]], axis=1)
+        main, cross = mm_tn(both, hi), mm_tn(both, lo)
+        gram = gram + (main[:RK] + (main[RK:] + cross[:RK] + cross[RK:]))
     for get in get_right:
         get.start()
     for half in range(2):
@@ -235,7 +236,7 @@
         o_all[at, :] = o
         o_hi[at, :], o_lo[at, :] = split(o)
     cross = mm_tn(o_hi[...], o_lo[...])
-    gram = (mm_tn(o_hi[...], o_hi[...]) + (cross + cross.T)) * norm
+    gram = (mm_tn(o_hi[...], o_hi[...]) + (cross + cross.T + mm_tn(o_lo[...], o_lo[...]))) * norm
     for half in range(2):
         src2[16 * half : 16 * half + 16, 0:8] = gram[0:128, 128 * half : 128 * half + 128].reshape(16, 8, 128)
     for k in range(32):
@@ -261,8 +262,7 @@
             y = mm(jnp.concatenate([x_hi, x_lo], axis=1), weights)
             lout[at, :] = y[:, :128] + y[:, 128:]
 
-    finish2 = exchange(sizes, src2, sum2, rx2, rz2, sems2, (invert, place_right, make_left))
-    g2_ref[...] = sum2[...]
+    finish2 = exchange(sizes, src2, g2_ref, rx2, rz2, sems2, (invert, place_right, make_left))
     finish1()
     finish2()
 
@@ -290,7 +290,8 @@
             pltpu.VMEM((out_rows, 256), BF16),
             pltpu.VMEM((out_rows, 256), F32),
             pltpu.VMEM((128, 256), F32),
-            *[pltpu.VMEM((lead, high, 128), F32) for high in (8, 12) for lead in (n, n, n - 1, nz)],
+            *[pltpu.VMEM((lead, 8, 128), F32) for lead in (n, n, n - 1, nz)],
+            *[pltpu.VMEM((lead, 12, 128), F32) for lead in (n, n - 1, nz)],
             pltpu.SemaphoreType.DMA((6,)),
             pltpu.SemaphoreType.DMA((6,)),
             pltpu.SemaphoreType.DMA((6,)),

time: 52.6 us -> 53.5 us (1.017)
  Pallas kernels: 51.7 us -> 52.6 us
    pallas_call x1, Pallas kernels: 45.1 us -> 46.1 us  [whole(): pl.pallas_call(functools.partial(whole_kernel, sizes, points, root, norm)...]
where the time goes in v8:
time: 53.5 us; the launch traced here: 53.4 us
  Pallas kernels  52.6 us (98%)
  between operations  0.8 us (1%)
    pallas_call x1, Pallas kernels, whole(): pl.pallas_call(functools.partial(whole_kernel, sizes, points, root, norm)...  46.1 us
    pallas_call x1, Pallas kernels, factor_and_place(): pl.pallas_call(factor_kernel, out_shape=(jax.ShapeDtypeStruct((256, 256),...  6.55 us

profile of v8, /device:TPU:1, one launch (start us, length us, event | category | flops | bytes accessed | tf_op | source)
XLA Modules:
  0.0 53.4 jit_solution(11977558588759996677)
XLA Ops:
  0.6 46.1 %whole.1 = (f32[4096,128]{1,0:T(8,128)S(1)}, f32[2,2048,128]{2,1,0:T(8,128)S(1)}, f32[32,12,128]{2,1,0:T(8,128)S(1)}) custom-call(f32[4096,256]{1,0:T(8,128)} %bitcast.4, f32[4096,256]{1,0:T(8,128)} %bitcast.5), custom_call_target="tpu_custom_call" | custom-call | tf_op jit(solution)/shard_map/whole/pallas_call | solution.py:275
  46.7 6.6 %factor_and_place.1 = (f32[256,256]{1,0:T(8,128)}, f32[4096,128]{1,0:T(8,128)}, f32[2048,256]{1,0:T(8,128)}) custom-call(f32[32,12,128]{2,1,0:T(8,128)S(1)} %get-tuple-element.9.g_ref, f32[4096,128]{1,0:T(8,128)S(1)} %get-tuple-element.10.lo_in, f32[2,2048,128]{2,1,0:T(8,128)S(1)} %get-tuple-element.11.ro_in), custom_call_target="tpu_custom_call" | custom-call | tf_op jit(solution)/shard_map/factor_and_place/pallas_call | solution.py:334

commit v9 on v8

--- a/solution.py
+++ b/solution.py
@@ -303,7 +303,7 @@
     )(left, right)
 
 
-def factor_kernel(g_ref, lo_in, ro_in, f_ref, lo_out, ro_out, work, corner, sem):
+def factor_kernel(g_ref, lo_in, ro_in, f_out, lo_out, ro_out, f_ref, work, corner, sem):
     puts = [pltpu.make_async_copy(lo_in, lo_out, sem.at[2])]
     for h in range(2):
         puts.append(pltpu.make_async_copy(ro_in.at[h], ro_out.at[:, 128 * h : 128 * h + 128], sem.at[h]))
@@ -317,13 +317,19 @@
     right = work[:, 128:256]
     f_ref[0:128, 0:128] = jnp.where(upper_mask(), work[:, 0:128], 0.0)
     f_ref[0:128, 128:256] = right
+    f_ref[128:256, 0:128] = jnp.zeros((128, 128), F32)
+    parts = [(pl.ds(0, 128), pl.ds(0, 256)), (pl.ds(128, 128), pl.ds(0, 128)), (pl.ds(128, 128), pl.ds(128, 128))]
+    for i, at in enumerate(parts):
+        puts.append(pltpu.make_async_copy(f_ref.at[at], f_out.at[at], sem.at[3 + i]))
+    for put in puts[-3:-1]:
+        put.start()
     update = lax.dot_general(
         right, right, (((0,), (0,)), ((), ())), precision=lax.Precision.HIGHEST, preferred_element_type=F32
     )
     work[:, 0:128] = corner[...] - update
     eliminate(work, 1)
-    f_ref[128:256, 0:128] = jnp.zeros((128, 128), F32)
     f_ref[128:256, 128:256] = jnp.where(upper_mask(), work[:, 0:128], 0.0)
+    puts[-1].start()
     for put in puts:
         put.wait()
 
@@ -339,8 +345,13 @@
             jax.ShapeDtypeStruct((right_out.shape[1], 256), F32),
         ),
         in_specs=[vmem_spec] * 3,
-        out_specs=(vmem_spec, hbm_spec, hbm_spec),
-        scratch_shapes=[pltpu.VMEM((128, 256), F32), pltpu.VMEM((128, 128), F32), pltpu.SemaphoreType.DMA((3,))],
+        out_specs=(hbm_spec, hbm_spec, hbm_spec),
+        scratch_shapes=[
+            pltpu.VMEM((256, 256), F32),
+            pltpu.VMEM((128, 256), F32),
+            pltpu.VMEM((128, 128), F32),
+            pltpu.SemaphoreType.DMA((6,)),
+        ],
         compiler_params=pltpu.CompilerParams(vmem_limit_bytes=8 << 20),
         name="factor_and_place",
     )(gram, left_out, right_out)

time: 53.5 us -> 53.5 us (level)
  no operation moved by 1% of the time
where the time goes in v9:
time: 53.5 us; the launch traced here: 53.4 us
  Pallas kernels  52.6 us (98%)
  between operations  0.8 us (1%)
    pallas_call x1, Pallas kernels, whole(): pl.pallas_call(functools.partial(whole_kernel, sizes, points, root, norm)...  46.1 us
    pallas_call x1, Pallas kernels, factor_and_place(): pl.pallas_call(factor_kernel, out_shape=(jax.ShapeDtypeStruct((256, 256),...  6.51 us

profile of v9, /device:TPU:1, one launch (start us, length us, event | category | flops | bytes accessed | tf_op | source)
XLA Modules:
  0.0 53.4 jit_solution(8255326595248794477)
XLA Ops:
  0.6 46.1 %whole.1 = (f32[4096,128]{1,0:T(8,128)S(1)}, f32[2,2048,128]{2,1,0:T(8,128)S(1)}, f32[32,12,128]{2,1,0:T(8,128)S(1)}) custom-call(f32[4096,256]{1,0:T(8,128)} %bitcast.4, f32[4096,256]{1,0:T(8,128)} %bitcast.5), custom_call_target="tpu_custom_call" | custom-call | tf_op jit(solution)/shard_map/whole/pallas_call | solution.py:275
  46.7 6.5 %factor_and_place.1 = (f32[256,256]{1,0:T(8,128)}, f32[4096,128]{1,0:T(8,128)}, f32[2048,256]{1,0:T(8,128)}) custom-call(f32[32,12,128]{2,1,0:T(8,128)S(1)} %get-tuple-element.9.g_ref, f32[4096,128]{1,0:T(8,128)S(1)} %get-tuple-element.10.lo_in, f32[2,2048,128]{2,1,0:T(8,128)S(1)} %get-tuple-element.11.ro_in), custom_call_target="tpu_custom_call" | custom-call | tf_op jit(solution)/shard_map/factor_and_place/pallas_call | solution.py:340
